TPU v7x, 32 devices: a whole 2x2x4 slice. The times are simulated.
32 devices in a mesh: ta: 4 (over x, core), au: 8 (over z, y).
Axes of the slice: x: 2, y: 2, z: 4, core: 2. Of those that a mesh axis runs over, the one named last changes fastest.
Arguments:
- embeddings: bfloat16 [786432, 192], P(('ta', 'au')), may hold values from -6 to 6
- stream_ids: int32 [786432], P(('ta', 'au')), may hold values from 0 to 63, never falling along the last dimension, each value on 1 to 24576 neighbouring positions
- start_block: bfloat16 [786432, 64], P(('ta', 'au')), may hold values from -6 to 6
Outputs:
- basis_rows: float32 [786432, 64], P(('ta', 'au'))
- ritz_matrix: float32 [64, 64], replicated
Inputs may be any that keep to these rules, and one draw needn't show every extreme that they name: stream_ids never fall along the rows; each stream holds 1 to 24576 rows.
All inputs are finite; a program needn't handle non-finite values.
Results may differ from a plain program's by a relative error of at most 0.0015.
Values may be sent and summed in bfloat16 or wider, within the bound.
No kernel may reach another device: no remote copies, remote signals or barrier semaphores. Data moves between devices by JAX's collectives and lax.ppermute only.
A program may use at most 192 MiB of HBM per device.

v0:
```python
import jax
import jax.numpy as jnp
from jax import lax
from jax.experimental import pallas as pl
from jax.experimental.pallas import tpu as pltpu
from jax.sharding import PartitionSpec as P

BAND = 128
HALO_BLOCKS = 5
HALO = HALO_BLOCKS * BAND
EMB = 192
VECS = 64
CHUNK_BLOCKS = 16
CHUNK = CHUNK_BLOCKS * BAND
DEPTH = 256
PENALTY = 64.0
EXPONENT = 4.328085122666891
VMEM_BYTES = 62 << 20

bf16 = jnp.bfloat16
f32 = jnp.float32


def columns(start, size):
    return pl.ds(pl.multiple_of(start, BAND), size)


def split(x):
    high = x.astype(bf16)
    return high, (x - high.astype(f32)).astype(bf16)


def prepare(values, labels, slot, lhs_ref, rhs_ref):
    width = values.shape[1]
    values = values.astype(f32)
    normed = (values * lax.rsqrt(jnp.sum(values * values, axis=0, keepdims=True) + 1e-06)).astype(bf16)
    shift = lax.broadcasted_iota(jnp.int32, (16, width), 0)
    bits = (lax.shift_right_logical(jnp.broadcast_to(labels, (16, width)), shift) & 1).astype(f32)
    unset = 1.0 - bits
    first = jnp.where(shift == 0, 1.0, 0.0)
    zeros = jnp.zeros((16, width), bf16)
    rhs = jnp.concatenate(
        [normed, (-PENALTY * unset).astype(bf16), (-PENALTY * bits).astype(bf16), (-first).astype(bf16), zeros], axis=0
    )
    lhs = jnp.concatenate([normed, bits.astype(bf16), unset.astype(bf16), first.astype(bf16), zeros], axis=0)
    rhs_ref[:, slot * BAND : slot * BAND + width] = rhs
    lhs_ref[slot * BAND : slot * BAND + width, :] = lhs.T


def affinity_pair(slot, block, carried, right, lhs_ref, rhs_ref, weight_ref, scale_ref):
    row = lax.broadcasted_iota(jnp.int32, (BAND, BAND), 0)
    col = lax.broadcasted_iota(jnp.int32, (BAND, BAND), 1)
    here = slice(slot * BAND, (slot + 2) * BAND)
    z = jnp.dot(lhs_ref[here, :], rhs_ref[:, here], preferred_element_type=f32)
    e = jnp.exp2(z * EXPONENT)
    own0 = e[:BAND, :BAND].astype(bf16)
    own1 = e[BAND:, BAND:].astype(bf16)
    right0 = jnp.where(row <= col, e[BAND:, :BAND], 0.0).astype(bf16)
    left1 = jnp.where(row >= col, e[:BAND, BAND:], 0.0).astype(bf16)
    weight_ref[block, BAND : 2 * BAND, :] = own0
    weight_ref[block, 2 * BAND :, :] = right0
    weight_ref[block + 1, :BAND, :] = left1
    weight_ref[block + 1, BAND : 2 * BAND, :] = own1
    sum0 = jnp.sum(own0.astype(f32) + right0.astype(f32), axis=0, keepdims=True) + carried
    scale_ref[:, columns(block * BAND, BAND)] = lax.rsqrt(sum0)
    if not right:
        return carried
    z = jnp.dot(
        lhs_ref[(slot + 2) * BAND : (slot + 3) * BAND, :],
        rhs_ref[:, (slot + 1) * BAND : (slot + 2) * BAND],
        preferred_element_type=f32,
    )
    right1 = jnp.where(row <= col, jnp.exp2(z * EXPONENT), 0.0).astype(bf16)
    left2 = right1.T
    weight_ref[block + 1, 2 * BAND :, :] = right1
    weight_ref[block + 2, :BAND, :] = left2
    sum1 = jnp.sum(own1.astype(f32) + left1.astype(f32) + right1.astype(f32), axis=0, keepdims=True)
    scale_ref[:, columns(block * BAND + BAND, BAND)] = lax.rsqrt(sum1)
    return jnp.sum(left2.astype(f32), axis=0, keepdims=True)


def filter_kernel(
    low_ref, high_ref, emb_ref, id_ref, start_hbm,
    level_hbm, gram_ref,
    lhs_ref, rhs_ref, weight_ref, scale_ref, carry_ref, start_ref, pack_a, pack_b, level_a, level_b, sum_ref, sems,
):
    step = pl.program_id(0)
    count = pl.num_programs(0)
    rows = count * CHUNK
    blocks = rows // BAND
    start_copy = pltpu.make_async_copy(start_hbm, start_ref.at[:, HALO : HALO + start_hbm.shape[1]], sems.at[0])

    def pairs(first_slot, first_block, number, last_right):
        carried = carry_ref[...]
        for i in range(number):
            right = last_right or i < number - 1
            carried = affinity_pair(
                first_slot + 2 * i, first_block + 2 * i, carried, right, lhs_ref, rhs_ref, weight_ref, scale_ref
            )
        carry_ref[...] = carried

    def halo(ref, slot):
        for begin, width in ((0, 256), (256, 256), (512, 128)):
            labels = ref[EMB + VECS : EMB + VECS + 16, begin : begin + width].astype(f32)[:1].astype(jnp.int32)
            prepare(ref[:EMB, begin : begin + width], labels, slot + begin // BAND, lhs_ref, rhs_ref)

    def keep_last():
        lhs_ref[:BAND, :] = lhs_ref[CHUNK:, :]
        rhs_ref[:, :BAND] = rhs_ref[:, CHUNK:]

    @pl.when(step == 0)
    def _():
        start_copy.start()
        carry_ref[...] = jnp.zeros_like(carry_ref)
        sum_ref[...] = jnp.zeros_like(sum_ref)
        start_ref[:, :HALO] = low_ref[EMB : EMB + VECS, :]
        start_ref[:, HALO + start_hbm.shape[1] :] = high_ref[EMB : EMB + VECS, :]
        halo(low_ref, CHUNK_BLOCKS + 1 - HALO_BLOCKS)
        pairs(CHUNK_BLOCKS + 1 - HALO_BLOCKS, 0, (HALO_BLOCKS - 1) // 2, True)
        keep_last()

    for j in range(CHUNK // 256):
        here = slice(j * 256, j * 256 + 256)
        prepare(emb_ref[:, here], id_ref[:, here] + 1, 1 + 2 * j, lhs_ref, rhs_ref)
    pairs(0, HALO_BLOCKS - 1 + step * CHUNK_BLOCKS, CHUNK_BLOCKS // 2, True)
    keep_last()

    @pl.when(step == count - 1)
    def _():
        halo(high_ref, 1)
        pairs(0, HALO_BLOCKS - 1 + blocks, (HALO_BLOCKS + 1) // 2, False)
        start_copy.wait()

        def loop(first, number, unroll, one):
            def body(i, carry):
                for u in range(unroll):
                    one(first + i * unroll + u)
                return carry

            lax.fori_loop(0, number // unroll, body, 0)

        def pack0(b):
            here = columns(b * BAND, BAND)
            pack_a[:, here] = (scale_ref[:, here] * start_ref[:, here].astype(f32)).astype(bf16)

        def operate(packed, b):
            product = jnp.dot(packed[:, columns((b - 1) * BAND, 3 * BAND)], weight_ref[b], preferred_element_type=f32)
            return scale_ref[:, columns(b * BAND, BAND)] * product

        def level1(b):
            here = columns(b * BAND, BAND)
            new = operate(pack_a, b) * (1.0 / 0.6) - 0.5 * start_ref[:, here].astype(f32)
            level_a[:, here] = new
            pack_b[:, here] = (scale_ref[:, here] * new).astype(bf16)

        def level2(b):
            here = columns(b * BAND, BAND)
            new = operate(pack_b, b) * (2.0 / 0.6) - level_a[:, here] - start_ref[:, here].astype(f32)
            level_b[:, here] = new
            pack_a[:, here] = (scale_ref[:, here] * new).astype(bf16)

        def level3(b):
            here = columns(b * BAND, BAND)
            new = operate(pack_a, b) * (2.0 / 0.6) - level_b[:, here] - level_a[:, here]
            level_a[:, here] = new
            pack_b[:, here] = (scale_ref[:, here] * new).astype(bf16)

        loop(1, blocks + 8, 20, pack0)
        loop(2, blocks + 6, 18, level1)
        loop(3, blocks + 4, 14, level2)
        loop(3, blocks + 4, 14, level3)
        out_copy = pltpu.make_async_copy(level_a.at[:, HALO : HALO + level_hbm.shape[1]], level_hbm, sems.at[1])
        out_copy.start()

        def grams(i, carry):
            first = HALO_BLOCKS + i * CHUNK_BLOCKS
            image = jnp.concatenate([operate(pack_b, first + u) for u in range(CHUNK_BLOCKS)], axis=1)
            high, low = split(level_a[:, columns(first * BAND, CHUNK)])
            left = jnp.concatenate([high, low], axis=0)
            right = jnp.concatenate([high, low, *split(image)], axis=0)
            sum_ref[...] += lax.dot_general(left, right, (((1,), (1,)), ((), ())), preferred_element_type=f32)
            return carry

        lax.fori_loop(0, count, grams, 0)
        total = sum_ref[:VECS, :] + sum_ref[VECS:, :]
        gram = total[:, :VECS] + total[:, VECS : 2 * VECS]
        image = total[:, 2 * VECS : 3 * VECS] + total[:, 3 * VECS :]
        gram_ref[...] = jnp.concatenate([gram, image], axis=1)
        out_copy.wait()


def filtered(low, high, emb, ids, start):
    rows = emb.shape[1]
    blocks = rows // BAND + 2 * HALO_BLOCKS
    whole = pl.BlockSpec(memory_space=pltpu.VMEM)
    return pl.pallas_call(
        filter_kernel,
        grid=(rows // CHUNK,),
        in_specs=[
            whole,
            whole,
            pl.BlockSpec((EMB, CHUNK), lambda i: (0, i)),
            pl.BlockSpec((1, CHUNK), lambda i: (0, i)),
            pl.BlockSpec(memory_space=pl.ANY),
        ],
        out_specs=[pl.BlockSpec(memory_space=pl.ANY), whole],
        out_shape=[
            jax.ShapeDtypeStruct((VECS, rows), f32),
            jax.ShapeDtypeStruct((VECS, 2 * VECS), f32),
        ],
        scratch_shapes=[
            pltpu.VMEM((CHUNK + BAND, DEPTH), bf16),
            pltpu.VMEM((DEPTH, CHUNK + BAND), bf16),
            pltpu.VMEM((blocks, 3 * BAND, BAND), bf16),
            pltpu.VMEM((1, blocks * BAND), f32),
            pltpu.VMEM((1, BAND), f32),
            pltpu.VMEM((VECS, blocks * BAND), bf16),
            pltpu.VMEM((VECS, blocks * BAND), bf16),
            pltpu.VMEM((VECS, blocks * BAND), bf16),
            pltpu.VMEM((VECS, blocks * BAND), f32),
            pltpu.VMEM((VECS, blocks * BAND), f32),
            pltpu.VMEM((2 * VECS, 4 * VECS), f32),
            pltpu.SemaphoreType.DMA((2,)),
        ],
        compiler_params=pltpu.CompilerParams(vmem_limit_bytes=VMEM_BYTES, dimension_semantics=("arbitrary",)),
        name="filter",
    )(low, high, emb, ids, start)


def basis_kernel(gram_ref, level_ref, basis_ref, ritz_ref, inverse_ref):
    @pl.when(pl.program_id(0) == 0)
    def _():
        row = lax.broadcasted_iota(jnp.int32, (VECS, 2 * VECS), 0)
        col = lax.broadcasted_iota(jnp.int32, (VECS, 2 * VECS), 1)
        work = jnp.where(col < VECS, gram_ref[...], jnp.where(col == row + VECS, 1.0, 0.0))
        for k in range(VECS - 1):
            pivot = work[k : k + 1, :]
            scaled = pivot / jnp.broadcast_to(pivot[:, k : k + 1], pivot.shape)
            factor = jnp.where(row > k, jnp.broadcast_to(work[:, k : k + 1], work.shape), 0.0)
            work = work - factor * scaled
        diagonal = jnp.sum(jnp.where(row == col, work, 0.0), axis=1, keepdims=True)
        inverse = (work * lax.rsqrt(diagonal))[:, VECS:]
        image = gram_ref[:, VECS:]
        exact = lax.Precision.HIGHEST
        left = jnp.dot(inverse, image, precision=exact, preferred_element_type=f32)
        ritz_ref[...] = lax.dot_general(
            left, inverse, (((1,), (1,)), ((), ())), precision=exact, preferred_element_type=f32
        )
        high, low = split(inverse)
        inverse_ref[...] = jnp.concatenate([high, high, low], axis=1)

    high, low = split(level_ref[...])
    basis_ref[...] = jnp.dot(
        inverse_ref[...], jnp.concatenate([high, low, high], axis=0), preferred_element_type=f32
    )


def orthonormal(sums, level):
    rows = level.shape[1]
    whole = pl.BlockSpec(memory_space=pltpu.VMEM)
    return pl.pallas_call(
        basis_kernel,
        grid=(rows // CHUNK,),
        in_specs=[whole, pl.BlockSpec((VECS, CHUNK), lambda i: (0, i))],
        out_specs=[pl.BlockSpec((VECS, CHUNK), lambda i: (0, i)), whole],
        out_shape=[
            jax.ShapeDtypeStruct((VECS, rows), f32),
            jax.ShapeDtypeStruct((VECS, VECS), f32),
        ],
        scratch_shapes=[pltpu.VMEM((VECS, 3 * VECS), bf16)],
        name="basis",
    )(sums, level)


def per_device(embeddings, stream_ids, start_block):
    emb, start = embeddings.T, start_block.T
    rows = emb.shape[1]
    ids = stream_ids.reshape(1, rows)

    def edge(begin):
        here = slice(begin, begin + HALO)
        labels = jnp.broadcast_to((ids[:, here] + 1).astype(bf16), (16, HALO))
        return jnp.concatenate([emb[:, here], start[:, here], labels], axis=0)

    axes = ("ta", "au")
    last = lax.axis_size(axes) - 1
    up = [(i, i + 1) for i in range(last)]
    down = [(i + 1, i) for i in range(last)]
    low = lax.ppermute(edge(rows - HALO), axes, up)
    high = lax.ppermute(edge(0), axes, down)
    level, sums = filtered(low, high, emb, ids, start)
    basis, ritz = orthonormal(lax.psum(sums, axes), level)
    return basis.T, ritz


def solution(mesh):
    placed = (P(("ta", "au"), None), P(("ta", "au")), P(("ta", "au"), None))
    return jax.shard_map(
        per_device,
        mesh=mesh,
        in_specs=placed,
        out_specs=(P(("ta", "au"), None), P()),
        check_vma=False,
    )
```

profile of v0, /device:TPU:0, one launch (start us, length us, event | category | flops | bytes accessed | tf_op | source)
XLA Modules:
  0.0 128.0 jit_solution(2598501979404965439)
XLA Ops:
  0.6 0.7 fusion.1
  1.4 0.9 fusion.5
  2.3 1.1 fusion.4
  3.5 4.9 %collective-permute-start = (bf16[272,640]{1,0:T(8,128)(2,1)S(1)}, bf16[272,640]{1,0:T(8,128)(2,1)S(1)}, u32[]{:S(2)}, u32[]{:S(2)}) collective-permute-start(bf16[272,640]{1,0:T(8,128)(2,1)S(1)} %pad_maximum_fusion), channel_id=1, source_target_pairs={{0,1},{1,2},{2,3},{3,4},{4,5},{5,6},{6,7},{7,8},{8,9},{9,10},{10,1... | collective-permute-start | bytes 1044488 | tf_op jit(solution)/shard_map/ppermute | solution.py:289
  8.4 1.3 %collective-permute-start.1 = (bf16[272,640]{1,0:T(8,128)(2,1)S(1)}, bf16[272,640]{1,0:T(8,128)(2,1)S(1)}, u32[]{:S(2)}, u32[]{:S(2)}) collective-permute-start(bf16[272,640]{1,0:T(8,128)(2,1)S(1)} %pad_maximum_fusion.1), channel_id=1, source_target_pairs={{1,0},{2,1},{3,2},{4,3},{5,4},{6,5},{7,6},{8,7},{9,8},{10,9},{11,1... | collective-permute-start | bytes 1044488 | tf_op jit(solution)/shard_map/ppermute | solution.py:290
  9.7 13.5 %collective-permute-done.low_ref = bf16[272,640]{1,0:T(8,128)(2,1)S(1)} collective-permute-done((bf16[272,640]{1,0:T(8,128)(2,1)S(1)}, bf16[272,640]{1,0:T(8,128)(2,1)S(1)}, u32[]{:S(2)}, u32[]{:S(2)}) %collective-permute-start) | collective-permute-done | bytes 348192 | tf_op jit(solution)/shard_map/ppermute | solution.py:289
  23.2 0.0 copy-start
  23.2 0.4 collective-permute-done.1.high_ref
  23.6 0.3 copy-done
  23.9 0.0 copy-start.1
  23.9 0.7 copy-done.1
  24.7 44.8 %filter.1 = (f32[64,24576]{1,0:T(8,128)}, f32[64,128]{1,0:T(8,128)}) custom-call(bf16[272,640]{1,0:T(8,128)(2,1)} %copy-done, bf16[272,640]{1,0:T(8,128)(2,1)} %copy-done.1, bf16[192,24576]{1,0:T(8,128)(2,1)} %bitcast.5, s32[1,24576]{1,0:T(1,128)} %bitcast.9, bf16[64,24576]{1,0:T(8,128)(2,1)} %bitcast.7), custom_call_target="tpu_custom_call" | custom-call | tf_op jit(solution)/shard_map/filter/pallas_call | solution.py:196
  69.5 42.3 %psum.7.gram_ref = f32[64,128]{1,0:T(8,128)} all-reduce(f32[64,128]{1,0:T(8,128)} %get-tuple-element.6), channel_id=1, replica_groups=mesh['ta'=4,'au'=8] {'ta','au'}, use_global_device_ids=true, to_apply=%region_0.0 | all-reduce | flops 8192 | bytes 65536 | tf_op jit(solution)/shard_map/psum | solution.py:292
  111.8 16.2 %basis.1 = (f32[64,24576]{1,0:T(8,128)}, f32[64,64]{1,0:T(8,128)}) custom-call(f32[64,128]{1,0:T(8,128)} %psum.7.gram_ref, f32[64,24576]{1,0:T(8,128)} %get-tuple-element.7.level_ref), custom_call_target="tpu_custom_call" | custom-call | tf_op jit(solution)/shard_map/basis/pallas_call | solution.py:261
  (4 shorter events, 0.1 us)
Async XLA Ops:
  3.5 19.7 %collective-permute-start = (bf16[272,640]{1,0:T(8,128)(2,1)S(1)}, bf16[272,640]{1,0:T(8,128)(2,1)S(1)}, u32[]{:S(2)}, u32[]{:S(2)}) collective-permute-start(bf16[272,640]{1,0:T(8,128)(2,1)S(1)} %pad_maximum_fusion), channel_id=1, source_target_pairs={{0,1},{1,2},{2,3},{3,4},{4,5},{5,6},{6,7},{7,8},{8,9},{9,10},{10,1... | collective-permute-start | bytes 1044488 | tf_op jit(solution)/shard_map/ppermute | solution.py:289
  8.4 15.2 %collective-permute-start.1 = (bf16[272,640]{1,0:T(8,128)(2,1)S(1)}, bf16[272,640]{1,0:T(8,128)(2,1)S(1)}, u32[]{:S(2)}, u32[]{:S(2)}) collective-permute-start(bf16[272,640]{1,0:T(8,128)(2,1)S(1)} %pad_maximum_fusion.1), channel_id=1, source_target_pairs={{1,0},{2,1},{3,2},{4,3},{5,4},{6,5},{7,6},{8,7},{9,8},{10,9},{11,1... | collective-permute-start | bytes 1044488 | tf_op jit(solution)/shard_map/ppermute | solution.py:290
  23.2 0.7 copy-start
  23.9 0.7 copy-start.1
where the time goes:
time: 129 us; the launch traced here: 128 us
  Pallas kernels  61 us (47%)
  blocking collectives  42.3 us (33%)
  waiting for transfers between devices  13.9 us (11%)
  starting transfers between devices  6.18 us (5%)
  local copies, waits for them, and re-layouts  3.1 us (2%)
    pallas_call x1, Pallas kernels, filtered(): pl.pallas_call(filter_kernel, grid=(rows // CHUNK,), in_specs=[whole, who...  44.8 us
    psum x1, blocking collectives, per_device(): basis, ritz = orthonormal(lax.psum(sums, axes), level)  42.3 us
    pallas_call x1, Pallas kernels, orthonormal(): pl.pallas_call(basis_kernel, grid=(rows // CHUNK,), in_specs=[whole, pl.B...  16.2 us
    ppermute x1, waiting for transfers between devices, per_device(): low = lax.ppermute(edge(rows - HALO), axes, up)  13.5 us
    ppermute x1, starting transfers between devices, per_device(): low = lax.ppermute(edge(rows - HALO), axes, up)  4.89 us
  transfers between devices with their start and end apart: 2, of which 2 were waited for; matrix products, arithmetic and copies ran while one was open for 0% of the time, Pallas kernels for 0%

commit v1 on v0

--- a/solution.py
+++ b/solution.py
@@ -79,131 +79,131 @@
     return jnp.sum(left2.astype(f32), axis=0, keepdims=True)
 
 
-def filter_kernel(
-    low_ref, high_ref, emb_ref, id_ref, start_hbm,
+def operators(lane, weight_ref, scale_ref, start_ref, pack_a, pack_b, level_a, level_b):
+    def at(b):
+        return columns(lane(b), BAND)
+
+    def pack0(b):
+        pack_a[:, at(b)] = (scale_ref[:, at(b)] * start_ref[:, at(b)].astype(f32)).astype(bf16)
+
+    def operate(packed, b):
+        window = packed[:, columns(lane(b - 1), 3 * BAND)]
+        return scale_ref[:, at(b)] * jnp.dot(window, weight_ref[b], preferred_element_type=f32)
+
+    def level1(b):
+        new = operate(pack_a, b) * (1.0 / 0.6) - 0.5 * start_ref[:, at(b)].astype(f32)
+        level_a[:, at(b)] = new
+        pack_b[:, at(b)] = (scale_ref[:, at(b)] * new).astype(bf16)
+
+    def level2(b):
+        new = operate(pack_b, b) * (2.0 / 0.6) - level_a[:, at(b)] - start_ref[:, at(b)].astype(f32)
+        level_b[:, at(b)] = new
+        pack_a[:, at(b)] = (scale_ref[:, at(b)] * new).astype(bf16)
+
+    def level3(b):
+        new = operate(pack_a, b) * (2.0 / 0.6) - level_b[:, at(b)] - level_a[:, at(b)]
+        level_a[:, at(b)] = new
+        pack_b[:, at(b)] = (scale_ref[:, at(b)] * new).astype(bf16)
+
+    def products(b, count):
+        image = jnp.concatenate([operate(pack_b, b + u) for u in range(count)], axis=1)
+        high, low = split(level_a[:, columns(lane(b), count * BAND)])
+        left = jnp.concatenate([high, low], axis=0)
+        right = jnp.concatenate([high, low, *split(image)], axis=0)
+        return lax.dot_general(left, right, (((1,), (1,)), ((), ())), preferred_element_type=f32)
+
+    return pack0, level1, level2, level3, products
+
+
+def combine(sums):
+    total = sums[:VECS, :] + sums[VECS:, :]
+    gram = total[:, :VECS] + total[:, VECS : 2 * VECS]
+    image = total[:, 2 * VECS : 3 * VECS] + total[:, 3 * VECS :]
+    return jnp.concatenate([gram, image], axis=1)
+
+
+def loop(first, number, unroll, one):
+    def body(i, carry):
+        for u in range(unroll):
+            one(first + i * unroll + u)
+        return carry
+
+    lax.fori_loop(0, number // unroll, body, 0)
+
+
+def unrolled(number, most):
+    return max(u for u in range(1, most + 1) if number % u == 0)
+
+
+def interior_kernel(
+    emb_ref, id_ref, start_hbm,
     level_hbm, gram_ref,
     lhs_ref, rhs_ref, weight_ref, scale_ref, carry_ref, start_ref, pack_a, pack_b, level_a, level_b, sum_ref, sems,
 ):
     step = pl.program_id(0)
     count = pl.num_programs(0)
-    rows = count * CHUNK
-    blocks = rows // BAND
-    start_copy = pltpu.make_async_copy(start_hbm, start_ref.at[:, HALO : HALO + start_hbm.shape[1]], sems.at[0])
-
-    def pairs(first_slot, first_block, number, last_right):
-        carried = carry_ref[...]
-        for i in range(number):
-            right = last_right or i < number - 1
-            carried = affinity_pair(
-                first_slot + 2 * i, first_block + 2 * i, carried, right, lhs_ref, rhs_ref, weight_ref, scale_ref
-            )
-        carry_ref[...] = carried
-
-    def halo(ref, slot):
-        for begin, width in ((0, 256), (256, 256), (512, 128)):
-            labels = ref[EMB + VECS : EMB + VECS + 16, begin : begin + width].astype(f32)[:1].astype(jnp.int32)
-            prepare(ref[:EMB, begin : begin + width], labels, slot + begin // BAND, lhs_ref, rhs_ref)
-
-    def keep_last():
-        lhs_ref[:BAND, :] = lhs_ref[CHUNK:, :]
-        rhs_ref[:, :BAND] = rhs_ref[:, CHUNK:]
+    own = weight_ref.shape[0] - 2
+    start_copy = pltpu.make_async_copy(start_hbm, start_ref.at[:, BAND:], sems.at[0])
 
     @pl.when(step == 0)
     def _():
         start_copy.start()
         carry_ref[...] = jnp.zeros_like(carry_ref)
         sum_ref[...] = jnp.zeros_like(sum_ref)
-        start_ref[:, :HALO] = low_ref[EMB : EMB + VECS, :]
-        start_ref[:, HALO + start_hbm.shape[1] :] = high_ref[EMB : EMB + VECS, :]
-        halo(low_ref, CHUNK_BLOCKS + 1 - HALO_BLOCKS)
-        pairs(CHUNK_BLOCKS + 1 - HALO_BLOCKS, 0, (HALO_BLOCKS - 1) // 2, True)
-        keep_last()
+        lhs_ref[:BAND, :] = jnp.zeros((BAND, DEPTH), bf16)
+        rhs_ref[:, :BAND] = jnp.zeros((DEPTH, BAND), bf16)
 
     for j in range(CHUNK // 256):
         here = slice(j * 256, j * 256 + 256)
         prepare(emb_ref[:, here], id_ref[:, here] + 1, 1 + 2 * j, lhs_ref, rhs_ref)
-    pairs(0, HALO_BLOCKS - 1 + step * CHUNK_BLOCKS, CHUNK_BLOCKS // 2, True)
-    keep_last()
+    carried = carry_ref[...]
+    for i in range(CHUNK_BLOCKS // 2):
+        carried = affinity_pair(
+            2 * i, step * CHUNK_BLOCKS + 2 * i, carried, True, lhs_ref, rhs_ref, weight_ref, scale_ref
+        )
+    carry_ref[...] = carried
+    lhs_ref[:BAND, :] = lhs_ref[CHUNK:, :]
+    rhs_ref[:, :BAND] = rhs_ref[:, CHUNK:]
 
     @pl.when(step == count - 1)
     def _():
-        halo(high_ref, 1)
-        pairs(0, HALO_BLOCKS - 1 + blocks, (HALO_BLOCKS + 1) // 2, False)
         start_copy.wait()
-
-        def loop(first, number, unroll, one):
-            def body(i, carry):
-                for u in range(unroll):
-                    one(first + i * unroll + u)
-                return carry
-
-            lax.fori_loop(0, number // unroll, body, 0)
-
-        def pack0(b):
-            here = columns(b * BAND, BAND)
-            pack_a[:, here] = (scale_ref[:, here] * start_ref[:, here].astype(f32)).astype(bf16)
-
-        def operate(packed, b):
-            product = jnp.dot(packed[:, columns((b - 1) * BAND, 3 * BAND)], weight_ref[b], preferred_element_type=f32)
-            return scale_ref[:, columns(b * BAND, BAND)] * product
-
-        def level1(b):
-            here = columns(b * BAND, BAND)
-            new = operate(pack_a, b) * (1.0 / 0.6) - 0.5 * start_ref[:, here].astype(f32)
-            level_a[:, here] = new
-            pack_b[:, here] = (scale_ref[:, here] * new).astype(bf16)
-
-        def level2(b):
-            here = columns(b * BAND, BAND)
-            new = operate(pack_b, b) * (2.0 / 0.6) - level_a[:, here] - start_ref[:, here].astype(f32)
-            level_b[:, here] = new
-            pack_a[:, here] = (scale_ref[:, here] * new).astype(bf16)
-
-        def level3(b):
-            here = columns(b * BAND, BAND)
-            new = operate(pack_a, b) * (2.0 / 0.6) - level_b[:, here] - level_a[:, here]
-            level_a[:, here] = new
-            pack_b[:, here] = (scale_ref[:, here] * new).astype(bf16)
-
-        loop(1, blocks + 8, 20, pack0)
-        loop(2, blocks + 6, 18, level1)
-        loop(3, blocks + 4, 14, level2)
-        loop(3, blocks + 4, 14, level3)
-        out_copy = pltpu.make_async_copy(level_a.at[:, HALO : HALO + level_hbm.shape[1]], level_hbm, sems.at[1])
+        pack0, level1, level2, level3, products = operators(
+            lambda b: b * BAND, weight_ref, scale_ref, start_ref, pack_a, pack_b, level_a, level_b
+        )
+        number = own - 2
+        loop(2, number, unrolled(number, 20), pack0)
+        loop(2, number, unrolled(number, 20), level1)
+        loop(2, number, unrolled(number, 20), level2)
+        loop(2, number, unrolled(number, 20), level3)
+        inner = slice((HALO_BLOCKS + 1) * BAND, (own + 1 - HALO_BLOCKS) * BAND)
+        outer = slice(HALO_BLOCKS * BAND, (own - HALO_BLOCKS) * BAND)
+        out_copy = pltpu.make_async_copy(level_a.at[:, inner], level_hbm.at[:, outer], sems.at[1])
         out_copy.start()
-
-        def grams(i, carry):
-            first = HALO_BLOCKS + i * CHUNK_BLOCKS
-            image = jnp.concatenate([operate(pack_b, first + u) for u in range(CHUNK_BLOCKS)], axis=1)
-            high, low = split(level_a[:, columns(first * BAND, CHUNK)])
-            left = jnp.concatenate([high, low], axis=0)
-            right = jnp.concatenate([high, low, *split(image)], axis=0)
-            sum_ref[...] += lax.dot_general(left, right, (((1,), (1,)), ((), ())), preferred_element_type=f32)
+        number = own - 2 * HALO_BLOCKS
+        group = unrolled(number, 16)
+
+        def body(i, carry):
+            sum_ref[...] += products(HALO_BLOCKS + 1 + i * group, group)
             return carry
 
-        lax.fori_loop(0, count, grams, 0)
-        total = sum_ref[:VECS, :] + sum_ref[VECS:, :]
-        gram = total[:, :VECS] + total[:, VECS : 2 * VECS]
-        image = total[:, 2 * VECS : 3 * VECS] + total[:, 3 * VECS :]
-        gram_ref[...] = jnp.concatenate([gram, image], axis=1)
+        lax.fori_loop(0, number // group, body, 0)
+        gram_ref[...] = combine(sum_ref[...])
         out_copy.wait()
 
 
-def filtered(low, high, emb, ids, start):
+def interior(emb, ids, start):
     rows = emb.shape[1]
-    blocks = rows // BAND + 2 * HALO_BLOCKS
-    whole = pl.BlockSpec(memory_space=pltpu.VMEM)
+    blocks = rows // BAND + 1
     return pl.pallas_call(
-        filter_kernel,
+        interior_kernel,
         grid=(rows // CHUNK,),
         in_specs=[
-            whole,
-            whole,
             pl.BlockSpec((EMB, CHUNK), lambda i: (0, i)),
             pl.BlockSpec((1, CHUNK), lambda i: (0, i)),
             pl.BlockSpec(memory_space=pl.ANY),
         ],
-        out_specs=[pl.BlockSpec(memory_space=pl.ANY), whole],
+        out_specs=[pl.BlockSpec(memory_space=pl.ANY), pl.BlockSpec(memory_space=pltpu.VMEM)],
         out_shape=[
             jax.ShapeDtypeStruct((VECS, rows), f32),
             jax.ShapeDtypeStruct((VECS, 2 * VECS), f32),
@@ -211,7 +211,7 @@
         scratch_shapes=[
             pltpu.VMEM((CHUNK + BAND, DEPTH), bf16),
             pltpu.VMEM((DEPTH, CHUNK + BAND), bf16),
-            pltpu.VMEM((blocks, 3 * BAND, BAND), bf16),
+            pltpu.VMEM((blocks + 1, 3 * BAND, BAND), bf16),
             pltpu.VMEM((1, blocks * BAND), f32),
             pltpu.VMEM((1, BAND), f32),
             pltpu.VMEM((VECS, blocks * BAND), bf16),
@@ -223,8 +223,116 @@
             pltpu.SemaphoreType.DMA((2,)),
         ],
         compiler_params=pltpu.CompilerParams(vmem_limit_bytes=VMEM_BYTES, dimension_semantics=("arbitrary",)),
-        name="filter",
-    )(low, high, emb, ids, start)
+        name="interior",
+    )(emb, ids, start)
+
+
+INSIDE = 2 * HALO
+ENDS = 2 * (HALO + INSIDE)
+END_BLOCKS = ENDS // BAND
+
+
+def ends_kernel(
+    low_ref, high_ref, id_ref, sums_ref, emb_hbm, start_hbm, level_in,
+    level_hbm, gram_ref,
+    emb_ref, lhs_ref, rhs_ref, weight_ref, scale_ref, start_ref, pack_a, pack_b, level_a, level_b, sems,
+):
+    rows = emb_hbm.shape[1]
+    first = slice(0, INSIDE)
+    last = slice(rows - INSIDE, rows)
+    first_at = slice(HALO, HALO + INSIDE)
+    last_at = slice(HALO + INSIDE, HALO + 2 * INSIDE)
+    copies = [
+        pltpu.make_async_copy(source.at[:, there], target.at[:, here], sems.at[i])
+        for i, (source, there, target, here) in enumerate(
+            (
+                (emb_hbm, first, emb_ref, first_at),
+                (emb_hbm, last, emb_ref, last_at),
+                (start_hbm, first, start_ref, first_at),
+                (start_hbm, last, start_ref, last_at),
+            )
+        )
+    ]
+    for copy in copies:
+        copy.start()
+    for ref, begin in ((low_ref, 0), (high_ref, ENDS - HALO)):
+        here = slice(begin, begin + HALO)
+        emb_ref[:, here] = ref[:EMB, :]
+        start_ref[:, here] = ref[EMB : EMB + VECS, :]
+    for copy in copies:
+        copy.wait()
+    for j in range(ENDS // 256):
+        here = slice(j * 256, j * 256 + 256)
+        prepare(emb_ref[:, here], id_ref[:, here], 2 * j, lhs_ref, rhs_ref)
+    carried = jnp.zeros((1, BAND), f32)
+    for i in range(END_BLOCKS // 2):
+        carried = affinity_pair(
+            2 * i, 2 * i, carried, i < END_BLOCKS // 2 - 1, lhs_ref, rhs_ref, weight_ref, scale_ref
+        )
+    pack0, level1, level2, level3, products = operators(
+        lambda b: b * BAND, weight_ref, scale_ref, start_ref, pack_a, pack_b, level_a, level_b
+    )
+    for margin, one in ((1, pack0), (2, level1), (3, level2), (4, level3)):
+        for b in range(margin, END_BLOCKS - margin):
+            one(b)
+    outs = [
+        pltpu.make_async_copy(level_a.at[:, here], level_hbm.at[:, there], sems.at[i])
+        for i, (here, there) in enumerate(
+            (
+                (slice(HALO, 2 * HALO), slice(0, HALO)),
+                (slice(ENDS - 2 * HALO, ENDS - HALO), slice(rows - HALO, rows)),
+            )
+        )
+    ]
+    for copy in outs:
+        copy.start()
+    sums = products(HALO_BLOCKS, HALO_BLOCKS) + products(END_BLOCKS - 2 * HALO_BLOCKS, HALO_BLOCKS)
+    gram_ref[...] = sums_ref[...] + combine(sums)
+    for copy in outs:
+        copy.wait()
+
+
+def ends(low, high, ids, sums, emb, start, level):
+    whole = pl.BlockSpec(memory_space=pltpu.VMEM)
+    away = pl.BlockSpec(memory_space=pl.ANY)
+    return pl.pallas_call(
+        ends_kernel,
+        in_specs=[whole, whole, whole, whole, away, away, away],
+        out_specs=[away, whole],
+        out_shape=[
+            jax.ShapeDtypeStruct(level.shape, f32),
+            jax.ShapeDtypeStruct((VECS, 2 * VECS), f32),
+        ],
+        input_output_aliases={6: 0},
+        scratch_shapes=[
+            pltpu.VMEM((EMB, ENDS), bf16),
+            pltpu.VMEM((ENDS, DEPTH), bf16),
+            pltpu.VMEM((DEPTH, ENDS), bf16),
+            pltpu.VMEM((END_BLOCKS, 3 * BAND, BAND), bf16),
+            pltpu.VMEM((1, ENDS), f32),
+            pltpu.VMEM((VECS, ENDS), bf16),
+            pltpu.VMEM((VECS, ENDS), bf16),
+            pltpu.VMEM((VECS, ENDS), bf16),
+            pltpu.VMEM((VECS, ENDS), f32),
+            pltpu.VMEM((VECS, ENDS), f32),
+            pltpu.SemaphoreType.DMA((4,)),
+        ],
+        compiler_params=pltpu.CompilerParams(vmem_limit_bytes=VMEM_BYTES),
+        name="ends",
+    )(low, high, ids, sums, emb, start, level)
+
+
+def total(x, axes):
+    for axis in axes:
+        size = lax.axis_size(axis)
+        if size & (size - 1):
+            x = lax.psum(x, axis)
+            continue
+        stride = 1
+        while stride < size:
+            x = x + lax.ppermute(x, axis, [(i, i ^ stride) for i in range(size)])
+            stride *= 2
+    return x
 
 
 def basis_kernel(gram_ref, level_ref, basis_ref, ritz_ref, inverse_ref):
@@ -288,8 +396,18 @@
     down = [(i + 1, i) for i in range(last)]
     low = lax.ppermute(edge(rows - HALO), axes, up)
     high = lax.ppermute(edge(0), axes, down)
-    level, sums = filtered(low, high, emb, ids, start)
-    basis, ritz = orthonormal(lax.psum(sums, axes), level)
+    level, sums = interior(emb, ids, start)
+    labels = jnp.concatenate(
+        [
+            low[EMB + VECS : EMB + VECS + 1, :].astype(jnp.int32),
+            ids[:, :INSIDE] + 1,
+            ids[:, rows - INSIDE :] + 1,
+            high[EMB + VECS : EMB + VECS + 1, :].astype(jnp.int32),
+        ],
+        axis=1,
+    )
+    level, sums = ends(low, high, labels, sums, emb, start, level)
+    basis, ritz = orthonormal(total(sums, axes), level)
     return basis.T, ritz
 
 

time: 129 us -> 101 us (0.78)
  blocking collectives: 42.3 us -> 0 us
  starting transfers between devices: 6.18 us -> 13.2 us
  Pallas kernels: 61 us -> 65.1 us
  other arithmetic: 0.8 us -> 3.62 us
    psum x1 -> x0, blocking collectives: 42.3 us -> none  [per_device(): basis, ritz = orthonormal(lax.psum(sums, axes), level)]
    ppermute x0 -> x5, waiting for transfers between devices: none -> 14.9 us  [total(): x = x + lax.ppermute(x, axis, [(i, i ^ stride) for i in range(size)])]
    ppermute x1, waiting for transfers between devices: 13.5 us -> 0.01 us  [per_device(): low = lax.ppermute(edge(rows - HALO), axes, up)]
    ppermute x0 -> x5, starting transfers between devices: none -> 7.03 us  [total(): x = x + lax.ppermute(x, axis, [(i, i ^ stride) for i in range(size)])]
    pallas_call x1 -> x2, Pallas kernels: 44.8 us -> 48.8 us  [the longest x1 41.9 us: interior(): pl.pallas_call(interior_kernel, grid=(rows // CHUNK,), in_specs=[pl.Block...]
    add x0 -> x6, other arithmetic: none -> 2.11 us  [the longest x5 1.39 us: total(): x = x + lax.ppermute(x, axis, [(i, i ^ stride) for i in range(size)])]
  transfers between devices with their start and end apart: 2 -> 7, of which waited for: 2 -> 5; matrix products, arithmetic and copies ran while one was open for 0% -> 1% of each run, Pallas kernels for 0% -> 42%
where the time goes in v1:
time: 101 us; the launch traced here: 99.7 us
  Pallas kernels  65.1 us (64%)
  waiting for transfers between devices  14.9 us (15%)
  starting transfers between devices  13.2 us (13%)
  other arithmetic  3.62 us (4%)
  local copies, waits for them, and re-layouts  2.16 us (2%)
    pallas_call x1, Pallas kernels, interior(): pl.pallas_call(interior_kernel, grid=(rows // CHUNK,), in_specs=[pl.Block...  41.9 us
    pallas_call x1, Pallas kernels, orthonormal(): pl.pallas_call(basis_kernel, grid=(rows // CHUNK,), in_specs=[whole, pl.B...  16.2 us
    ppermute x5, waiting for transfers between devices, total(): x = x + lax.ppermute(x, axis, [(i, i ^ stride) for i in range(size)])  14.9 us
    ppermute x5, starting transfers between devices, total(): x = x + lax.ppermute(x, axis, [(i, i ^ stride) for i in range(size)])  7.03 us
    pallas_call x1, Pallas kernels, ends(): pl.pallas_call(ends_kernel, in_specs=[whole, whole, whole, whole, away, a...  6.92 us
    ppermute x1, starting transfers between devices, per_device(): low = lax.ppermute(edge(rows - HALO), axes, up)  4.89 us
    slice x2, local copies, waits for them, and re-layouts, edge(): return jnp.concatenate([emb[:, here], start[:, here], labels], axis=0)  2.05 us
  transfers between devices with their start and end apart: 7, of which 5 were waited for; matrix products, arithmetic and copies ran while one was open for 1% of the time, Pallas kernels for 42%

profile of v1, /device:TPU:0, one launch (start us, length us, event | category | flops | bytes accessed | tf_op | source)
XLA Modules:
  0.0 99.7 jit_solution(13726207930420345084)
XLA Ops:
  0.6 0.7 fusion.1
  1.4 0.9 fusion.5
  2.3 1.1 %fusion.4 = (bf16[192,640]{1,0:T(8,128)(2,1)S(1)}, bf16[192,640]{1,0:T(8,128)(2,1)S(1)}) fusion(bf16[192,24576]{1,0:T(8,128)(2,1)} %bitcast.4), kind=kLoop, calls=%fused_computation.13 | loop fusion | bytes 983040 | tf_op jit(solution)/shard_map/slice | solution.py:391
  3.5 4.9 %collective-permute-start = (bf16[272,640]{1,0:T(8,128)(2,1)S(1)}, bf16[272,640]{1,0:T(8,128)(2,1)S(1)}, u32[]{:S(2)}, u32[]{:S(2)}) collective-permute-start(bf16[272,640]{1,0:T(8,128)(2,1)S(1)} %pad_maximum_fusion), channel_id=1, source_target_pairs={{0,1},{1,2},{2,3},{3,4},{4,5},{5,6},{6,7},{7,8},{8,9},{9,10},{10,1... | collective-permute-start | bytes 1044488 | tf_op jit(solution)/shard_map/ppermute | solution.py:397
  8.4 1.3 %collective-permute-start.1 = (bf16[272,640]{1,0:T(8,128)(2,1)S(1)}, bf16[272,640]{1,0:T(8,128)(2,1)S(1)}, u32[]{:S(2)}, u32[]{:S(2)}) collective-permute-start(bf16[272,640]{1,0:T(8,128)(2,1)S(1)} %pad_maximum_fusion.1), channel_id=1, source_target_pairs={{1,0},{2,1},{3,2},{4,3},{5,4},{6,5},{7,6},{8,7},{9,8},{10,9},{11,1... | collective-permute-start | bytes 1044488 | tf_op jit(solution)/shard_map/ppermute | solution.py:398
  9.7 0.7 slice_add_fusion.1
  10.4 41.9 %interior.1 = (f32[64,24576]{1,0:T(8,128)}, f32[64,128]{1,0:T(8,128)}) custom-call(bf16[192,24576]{1,0:T(8,128)(2,1)} %bitcast.5, s32[1,24576]{1,0:T(1,128)} %bitcast.12, bf16[64,24576]{1,0:T(8,128)(2,1)} %bitcast.8), custom_call_target="tpu_custom_call" | custom-call | tf_op jit(solution)/shard_map/interior/pallas_call | solution.py:198
  52.4 0.0 copy-start
  52.4 0.0 collective-permute-done.1.high_ref
  52.5 0.7 pad_add_fusion.id_ref
  53.2 0.1 copy-done.1
  53.2 6.9 %ends.1 = (f32[64,24576]{1,0:T(8,128)}, f32[64,128]{1,0:T(8,128)}) custom-call(bf16[272,640]{1,0:T(8,128)(2,1)} %copy-done, bf16[272,640]{1,0:T(8,128)(2,1)} %copy-done.1, s32[1,3840]{1,0:T(1,128)} %pad_add_fusion.id_ref, f32[64,128]{1,0:T(8,128)} %get-tuple-element.8.sums_ref, bf16[192,24576]{1,0:T(8,128)(2,1)} %bitcast.6, ...), custom_call_target="tpu_custom_call", output_to_operand_aliasing={{0}: (6, {})} | custom-call | tf_op jit(solution)/shard_map/ends/pallas_call | solution.py:298
  60.2 3.8 %collective-permute-start.2 = (f32[64,128]{1,0:T(8,128)}, f32[64,128]{1,0:T(8,128)S(1)}, u32[]{:S(2)}, u32[]{:S(2)}) collective-permute-start(f32[64,128]{1,0:T(8,128)} %get-tuple-element.10), channel_id=1, source_target_pairs={{0,8},{8,0},{16,24},{24,16},{1,9},{9,1},{17,25},{25,17},{2,10},{10... | collective-permute-start | bytes 98312 | tf_op jit(solution)/shard_map/ppermute | solution.py:333
  64.0 1.1 %collective-permute-done.2 = f32[64,128]{1,0:T(8,128)S(1)} collective-permute-done((f32[64,128]{1,0:T(8,128)}, f32[64,128]{1,0:T(8,128)S(1)}, u32[]{:S(2)}, u32[]{:S(2)}) %collective-permute-start.2) | collective-permute-done | bytes 32800 | tf_op jit(solution)/shard_map/ppermute | solution.py:333
  65.1 0.8 add.31
  65.8 2.5 %collective-permute-start.3 = (f32[64,128]{1,0:T(8,128)S(1)}, f32[64,128]{1,0:T(8,128)S(1)}, u32[]{:S(2)}, u32[]{:S(2)}) collective-permute-start(f32[64,128]{1,0:T(8,128)S(1)} %add.31), channel_id=1, source_target_pairs={{0,16},{8,24},{16,0},{24,8},{1,17},{9,25},{17,1},{25,9},{2,18},{10... | collective-permute-start | bytes 98312 | tf_op jit(solution)/shard_map/ppermute | solution.py:333
  68.3 1.9 %collective-permute-done.3 = f32[64,128]{1,0:T(8,128)S(1)} collective-permute-done((f32[64,128]{1,0:T(8,128)S(1)}, f32[64,128]{1,0:T(8,128)S(1)}, u32[]{:S(2)}, u32[]{:S(2)}) %collective-permute-start.3) | collective-permute-done | bytes 32800 | tf_op jit(solution)/shard_map/ppermute | solution.py:333
  70.2 3.9 %collective-permute-done.4 = f32[64,128]{1,0:T(8,128)S(1)} collective-permute-done((f32[64,128]{1,0:T(8,128)S(1)}, f32[64,128]{1,0:T(8,128)S(1)}, u32[]{:S(2)}, u32[]{:S(2)}) %collective-permute-start.4) | collective-permute-done | bytes 32800 | tf_op jit(solution)/shard_map/ppermute | solution.py:333
  74.1 0.0 collective-permute-start.5
  74.2 3.9 %collective-permute-done.5 = f32[64,128]{1,0:T(8,128)S(1)} collective-permute-done((f32[64,128]{1,0:T(8,128)S(1)}, f32[64,128]{1,0:T(8,128)S(1)}, u32[]{:S(2)}, u32[]{:S(2)}) %collective-permute-start.5) | collective-permute-done | bytes 32800 | tf_op jit(solution)/shard_map/ppermute | solution.py:333
  78.1 0.7 collective-permute-start.6
  78.8 4.1 %collective-permute-done.6 = f32[64,128]{1,0:T(8,128)S(1)} collective-permute-done((f32[64,128]{1,0:T(8,128)S(1)}, f32[64,128]{1,0:T(8,128)S(1)}, u32[]{:S(2)}, u32[]{:S(2)}) %collective-permute-start.6) | collective-permute-done | bytes 32800 | tf_op jit(solution)/shard_map/ppermute | solution.py:333
  82.9 0.6 add.35.gram_ref
  83.5 16.2 %basis.1 = (f32[64,24576]{1,0:T(8,128)}, f32[64,64]{1,0:T(8,128)}) custom-call(f32[64,128]{1,0:T(8,128)} %add.35.gram_ref, f32[64,24576]{1,0:T(8,128)} %get-tuple-element.11.level_ref), custom_call_target="tpu_custom_call" | custom-call | tf_op jit(solution)/shard_map/basis/pallas_call | solution.py:369
  (13 shorter events, 0.1 us)
Async XLA Ops:
  3.5 48.9 %collective-permute-start = (bf16[272,640]{1,0:T(8,128)(2,1)S(1)}, bf16[272,640]{1,0:T(8,128)(2,1)S(1)}, u32[]{:S(2)}, u32[]{:S(2)}) collective-permute-start(bf16[272,640]{1,0:T(8,128)(2,1)S(1)} %pad_maximum_fusion), channel_id=1, source_target_pairs={{0,1},{1,2},{2,3},{3,4},{4,5},{5,6},{6,7},{7,8},{8,9},{9,10},{10,1... | collective-permute-start | bytes 1044488 | tf_op jit(solution)/shard_map/ppermute | solution.py:397
  8.4 44.0 %collective-permute-start.1 = (bf16[272,640]{1,0:T(8,128)(2,1)S(1)}, bf16[272,640]{1,0:T(8,128)(2,1)S(1)}, u32[]{:S(2)}, u32[]{:S(2)}) collective-permute-start(bf16[272,640]{1,0:T(8,128)(2,1)S(1)} %pad_maximum_fusion.1), channel_id=1, source_target_pairs={{1,0},{2,1},{3,2},{4,3},{5,4},{6,5},{7,6},{8,7},{9,8},{10,9},{11,1... | collective-permute-start | bytes 1044488 | tf_op jit(solution)/shard_map/ppermute | solution.py:398
  52.4 0.8 copy-start
  52.4 0.8 copy-start.1
  60.2 4.9 %collective-permute-start.2 = (f32[64,128]{1,0:T(8,128)}, f32[64,128]{1,0:T(8,128)S(1)}, u32[]{:S(2)}, u32[]{:S(2)}) collective-permute-start(f32[64,128]{1,0:T(8,128)} %get-tuple-element.10), channel_id=1, source_target_pairs={{0,8},{8,0},{16,24},{24,16},{1,9},{9,1},{17,25},{25,17},{2,10},{10... | collective-permute-start | bytes 98312 | tf_op jit(solution)/shard_map/ppermute | solution.py:333
  65.8 4.4 %collective-permute-start.3 = (f32[64,128]{1,0:T(8,128)S(1)}, f32[64,128]{1,0:T(8,128)S(1)}, u32[]{:S(2)}, u32[]{:S(2)}) collective-permute-start(f32[64,128]{1,0:T(8,128)S(1)} %add.31), channel_id=1, source_target_pairs={{0,16},{8,24},{16,0},{24,8},{1,17},{9,25},{17,1},{25,9},{2,18},{10... | collective-permute-start | bytes 98312 | tf_op jit(solution)/shard_map/ppermute | solution.py:333
  70.2 3.9 %collective-permute-start.4 = (f32[64,128]{1,0:T(8,128)S(1)}, f32[64,128]{1,0:T(8,128)S(1)}, u32[]{:S(2)}, u32[]{:S(2)}) collective-permute-start(f32[64,128]{1,0:T(8,128)S(1)} %add.32), channel_id=1, source_target_pairs={{0,1},{1,0},{2,3},{3,2},{4,5},{5,4},{6,7},{7,6},{8,9},{9,8},{10,11... | collective-permute-start | bytes 98312 | tf_op jit(solution)/shard_map/ppermute | solution.py:333
  74.1 3.9 %collective-permute-start.5 = (f32[64,128]{1,0:T(8,128)S(1)}, f32[64,128]{1,0:T(8,128)S(1)}, u32[]{:S(2)}, u32[]{:S(2)}) collective-permute-start(f32[64,128]{1,0:T(8,128)S(1)} %add.33), channel_id=1, source_target_pairs={{0,2},{1,3},{2,0},{3,1},{4,6},{5,7},{6,4},{7,5},{8,10},{9,11},{10,... | collective-permute-start | bytes 98312 | tf_op jit(solution)/shard_map/ppermute | solution.py:333
  78.1 4.8 %collective-permute-start.6 = (f32[64,128]{1,0:T(8,128)S(1)}, f32[64,128]{1,0:T(8,128)S(1)}, u32[]{:S(2)}, u32[]{:S(2)}) collective-permute-start(f32[64,128]{1,0:T(8,128)S(1)} %add.34), channel_id=1, source_target_pairs={{0,4},{1,5},{2,6},{3,7},{4,0},{5,1},{6,2},{7,3},{8,12},{9,13},{10,... | collective-permute-start | bytes 98312 | tf_op jit(solution)/shard_map/ppermute | solution.py:333

commit v2 on v1

--- a/solution.py
+++ b/solution.py
@@ -44,14 +44,14 @@
     )
     lhs = jnp.concatenate([normed, bits.astype(bf16), unset.astype(bf16), first.astype(bf16), zeros], axis=0)
     rhs_ref[:, slot * BAND : slot * BAND + width] = rhs
-    lhs_ref[slot * BAND : slot * BAND + width, :] = lhs.T
+    lhs_ref[:, slot * BAND : slot * BAND + width] = lhs
 
 
 def affinity_pair(slot, block, carried, right, lhs_ref, rhs_ref, weight_ref, scale_ref):
     row = lax.broadcasted_iota(jnp.int32, (BAND, BAND), 0)
     col = lax.broadcasted_iota(jnp.int32, (BAND, BAND), 1)
     here = slice(slot * BAND, (slot + 2) * BAND)
-    z = jnp.dot(lhs_ref[here, :], rhs_ref[:, here], preferred_element_type=f32)
+    z = lax.dot_general(lhs_ref[:, here], rhs_ref[:, here], (((0,), (0,)), ((), ())), preferred_element_type=f32)
     e = jnp.exp2(z * EXPONENT)
     own0 = e[:BAND, :BAND].astype(bf16)
     own1 = e[BAND:, BAND:].astype(bf16)
@@ -65,9 +65,10 @@
     scale_ref[:, columns(block * BAND, BAND)] = lax.rsqrt(sum0)
     if not right:
         return carried
-    z = jnp.dot(
-        lhs_ref[(slot + 2) * BAND : (slot + 3) * BAND, :],
+    z = lax.dot_general(
+        lhs_ref[:, (slot + 2) * BAND : (slot + 3) * BAND],
         rhs_ref[:, (slot + 1) * BAND : (slot + 2) * BAND],
+        (((0,), (0,)), ((), ())),
         preferred_element_type=f32,
     )
     right1 = jnp.where(row <= col, jnp.exp2(z * EXPONENT), 0.0).astype(bf16)
@@ -108,17 +109,18 @@
     def products(b, count):
         image = jnp.concatenate([operate(pack_b, b + u) for u in range(count)], axis=1)
         high, low = split(level_a[:, columns(lane(b), count * BAND)])
-        left = jnp.concatenate([high, low], axis=0)
-        right = jnp.concatenate([high, low, *split(image)], axis=0)
+        left = jnp.concatenate([high, *split(image)], axis=0)
+        right = jnp.concatenate([high, low], axis=0)
         return lax.dot_general(left, right, (((1,), (1,)), ((), ())), preferred_element_type=f32)
 
     return pack0, level1, level2, level3, products
 
 
 def combine(sums):
-    total = sums[:VECS, :] + sums[VECS:, :]
-    gram = total[:, :VECS] + total[:, VECS : 2 * VECS]
-    image = total[:, 2 * VECS : 3 * VECS] + total[:, 3 * VECS :]
+    cross = sums[:VECS, VECS:]
+    gram = sums[:VECS, :VECS] + cross + cross.T
+    image = sums[VECS : 2 * VECS, :] + sums[2 * VECS :, :]
+    image = (image[:, :VECS] + image[:, VECS:]).T
     return jnp.concatenate([gram, image], axis=1)
 
 
@@ -136,23 +138,21 @@
 
 
 def interior_kernel(
-    emb_ref, id_ref, start_hbm,
+    emb_ref, id_ref, chunk_ref,
     level_hbm, gram_ref,
     lhs_ref, rhs_ref, weight_ref, scale_ref, carry_ref, start_ref, pack_a, pack_b, level_a, level_b, sum_ref, sems,
 ):
     step = pl.program_id(0)
     count = pl.num_programs(0)
     own = weight_ref.shape[0] - 2
-    start_copy = pltpu.make_async_copy(start_hbm, start_ref.at[:, BAND:], sems.at[0])
-
     @pl.when(step == 0)
     def _():
-        start_copy.start()
         carry_ref[...] = jnp.zeros_like(carry_ref)
         sum_ref[...] = jnp.zeros_like(sum_ref)
-        lhs_ref[:BAND, :] = jnp.zeros((BAND, DEPTH), bf16)
+        lhs_ref[:, :BAND] = jnp.zeros((DEPTH, BAND), bf16)
         rhs_ref[:, :BAND] = jnp.zeros((DEPTH, BAND), bf16)
 
+    start_ref[:, columns(step * CHUNK + BAND, CHUNK)] = chunk_ref[...]
     for j in range(CHUNK // 256):
         here = slice(j * 256, j * 256 + 256)
         prepare(emb_ref[:, here], id_ref[:, here] + 1, 1 + 2 * j, lhs_ref, rhs_ref)
@@ -162,26 +162,25 @@
             2 * i, step * CHUNK_BLOCKS + 2 * i, carried, True, lhs_ref, rhs_ref, weight_ref, scale_ref
         )
     carry_ref[...] = carried
-    lhs_ref[:BAND, :] = lhs_ref[CHUNK:, :]
+    lhs_ref[:, :BAND] = lhs_ref[:, CHUNK:]
     rhs_ref[:, :BAND] = rhs_ref[:, CHUNK:]
 
     @pl.when(step == count - 1)
     def _():
-        start_copy.wait()
         pack0, level1, level2, level3, products = operators(
             lambda b: b * BAND, weight_ref, scale_ref, start_ref, pack_a, pack_b, level_a, level_b
         )
         number = own - 2
-        loop(2, number, unrolled(number, 20), pack0)
-        loop(2, number, unrolled(number, 20), level1)
-        loop(2, number, unrolled(number, 20), level2)
-        loop(2, number, unrolled(number, 20), level3)
+        loop(2, number, unrolled(number, 100), pack0)
+        loop(2, number, unrolled(number, 100), level1)
+        loop(2, number, unrolled(number, 100), level2)
+        loop(2, number, unrolled(number, 100), level3)
         inner = slice((HALO_BLOCKS + 1) * BAND, (own + 1 - HALO_BLOCKS) * BAND)
         outer = slice(HALO_BLOCKS * BAND, (own - HALO_BLOCKS) * BAND)
-        out_copy = pltpu.make_async_copy(level_a.at[:, inner], level_hbm.at[:, outer], sems.at[1])
+        out_copy = pltpu.make_async_copy(level_a.at[:, inner], level_hbm.at[:, outer], sems)
         out_copy.start()
         number = own - 2 * HALO_BLOCKS
-        group = unrolled(number, 16)
+        group = unrolled(number, 26)
 
         def body(i, carry):
             sum_ref[...] += products(HALO_BLOCKS + 1 + i * group, group)
@@ -201,7 +200,7 @@
         in_specs=[
             pl.BlockSpec((EMB, CHUNK), lambda i: (0, i)),
             pl.BlockSpec((1, CHUNK), lambda i: (0, i)),
-            pl.BlockSpec(memory_space=pl.ANY),
+            pl.BlockSpec((VECS, CHUNK), lambda i: (0, i)),
         ],
         out_specs=[pl.BlockSpec(memory_space=pl.ANY), pl.BlockSpec(memory_space=pltpu.VMEM)],
         out_shape=[
@@ -209,7 +208,7 @@
             jax.ShapeDtypeStruct((VECS, 2 * VECS), f32),
         ],
         scratch_shapes=[
-            pltpu.VMEM((CHUNK + BAND, DEPTH), bf16),
+            pltpu.VMEM((DEPTH, CHUNK + BAND), bf16),
             pltpu.VMEM((DEPTH, CHUNK + BAND), bf16),
             pltpu.VMEM((blocks + 1, 3 * BAND, BAND), bf16),
             pltpu.VMEM((1, blocks * BAND), f32),
@@ -219,8 +218,8 @@
             pltpu.VMEM((VECS, blocks * BAND), bf16),
             pltpu.VMEM((VECS, blocks * BAND), f32),
             pltpu.VMEM((VECS, blocks * BAND), f32),
-            pltpu.VMEM((2 * VECS, 4 * VECS), f32),
-            pltpu.SemaphoreType.DMA((2,)),
+            pltpu.VMEM((3 * VECS, 2 * VECS), f32),
+            pltpu.SemaphoreType.DMA,
         ],
         compiler_params=pltpu.CompilerParams(vmem_limit_bytes=VMEM_BYTES, dimension_semantics=("arbitrary",)),
         name="interior",
@@ -306,7 +305,7 @@
         input_output_aliases={6: 0},
         scratch_shapes=[
             pltpu.VMEM((EMB, ENDS), bf16),
-            pltpu.VMEM((ENDS, DEPTH), bf16),
+            pltpu.VMEM((DEPTH, ENDS), bf16),
             pltpu.VMEM((DEPTH, ENDS), bf16),
             pltpu.VMEM((END_BLOCKS, 3 * BAND, BAND), bf16),
             pltpu.VMEM((1, ENDS), f32),
@@ -335,9 +334,13 @@
     return x
 
 
-def basis_kernel(gram_ref, level_ref, basis_ref, ritz_ref, inverse_ref):
+def basis_kernel(gram_ref, level_hbm, basis_ref, ritz_ref, inverse_ref, level_ref, sem):
+    width = basis_ref.shape[1]
+
     @pl.when(pl.program_id(0) == 0)
     def _():
+        copy = pltpu.make_async_copy(level_hbm, level_ref, sem)
+        copy.start()
         row = lax.broadcasted_iota(jnp.int32, (VECS, 2 * VECS), 0)
         col = lax.broadcasted_iota(jnp.int32, (VECS, 2 * VECS), 1)
         work = jnp.where(col < VECS, gram_ref[...], jnp.where(col == row + VECS, 1.0, 0.0))
@@ -356,8 +359,9 @@
         )
         high, low = split(inverse)
         inverse_ref[...] = jnp.concatenate([high, high, low], axis=1)
-
-    high, low = split(level_ref[...])
+        copy.wait()
+
+    high, low = split(level_ref[:, columns(pl.program_id(0) * width, width)])
     basis_ref[...] = jnp.dot(
         inverse_ref[...], jnp.concatenate([high, low, high], axis=0), preferred_element_type=f32
     )
@@ -365,17 +369,23 @@
 
 def orthonormal(sums, level):
     rows = level.shape[1]
+    width = 4 * CHUNK
     whole = pl.BlockSpec(memory_space=pltpu.VMEM)
     return pl.pallas_call(
         basis_kernel,
-        grid=(rows // CHUNK,),
-        in_specs=[whole, pl.BlockSpec((VECS, CHUNK), lambda i: (0, i))],
-        out_specs=[pl.BlockSpec((VECS, CHUNK), lambda i: (0, i)), whole],
+        grid=(rows // width,),
+        in_specs=[whole, pl.BlockSpec(memory_space=pl.ANY)],
+        out_specs=[pl.BlockSpec((VECS, width), lambda i: (0, i)), whole],
         out_shape=[
             jax.ShapeDtypeStruct((VECS, rows), f32),
             jax.ShapeDtypeStruct((VECS, VECS), f32),
         ],
-        scratch_shapes=[pltpu.VMEM((VECS, 3 * VECS), bf16)],
+        scratch_shapes=[
+            pltpu.VMEM((VECS, 3 * VECS), bf16),
+            pltpu.VMEM((VECS, rows), f32),
+            pltpu.SemaphoreType.DMA,
+        ],
+        compiler_params=pltpu.CompilerParams(vmem_limit_bytes=VMEM_BYTES),
         name="basis",
     )(sums, level)
 

time: 101 us -> 89.5 us (0.89)
  Pallas kernels: 65.1 us -> 54 us
    pallas_call x1, Pallas kernels: 16.2 us -> 10.5 us  [orthonormal(): pl.pallas_call(basis_kernel, grid=(rows // width,), in_specs=[whole, pl.B...]
    pallas_call x1, Pallas kernels: 41.9 us -> 36.5 us  [interior(): pl.pallas_call(interior_kernel, grid=(rows // CHUNK,), in_specs=[pl.Block...]
  transfers between devices with their start and end apart: 7 -> 7, of which waited for: 5 -> 5; matrix products, arithmetic and copies ran while one was open for 1% -> 1% of each run, Pallas kernels for 42% -> 41%
where the time goes in v2:
time: 89.5 us; the launch traced here: 88.8 us
  Pallas kernels  54 us (60%)
  waiting for transfers between devices  14.9 us (17%)
  starting transfers between devices  13.2 us (15%)
  other arithmetic  3.62 us (4%)
  local copies, waits for them, and re-layouts  2.16 us (2%)
  between operations  0.93 us (1%)
    pallas_call x1, Pallas kernels, interior(): pl.pallas_call(interior_kernel, grid=(rows // CHUNK,), in_specs=[pl.Block...  36.5 us
    ppermute x5, waiting for transfers between devices, total(): x = x + lax.ppermute(x, axis, [(i, i ^ stride) for i in range(size)])  14.9 us
    pallas_call x1, Pallas kernels, orthonormal(): pl.pallas_call(basis_kernel, grid=(rows // width,), in_specs=[whole, pl.B...  10.5 us
    ppermute x5, starting transfers between devices, total(): x = x + lax.ppermute(x, axis, [(i, i ^ stride) for i in range(size)])  7.04 us
    pallas_call x1, Pallas kernels, ends(): pl.pallas_call(ends_kernel, in_specs=[whole, whole, whole, whole, away, a...  7.01 us
    ppermute x1, starting transfers between devices, per_device(): low = lax.ppermute(edge(rows - HALO), axes, up)  4.89 us
    slice x2, local copies, waits for them, and re-layouts, edge(): return jnp.concatenate([emb[:, here], start[:, here], labels], axis=0)  2.05 us
  transfers between devices with their start and end apart: 7, of which 5 were waited for; matrix products, arithmetic and copies ran while one was open for 1% of the time, Pallas kernels for 41%

profile of v2, /device:TPU:0, one launch (start us, length us, event | category | flops | bytes accessed | tf_op | source)
XLA Modules:
  0.0 88.8 jit_solution(14217607124542348866)
XLA Ops:
  0.6 0.7 fusion.1
  1.4 0.9 %fusion.5 = (bf16[64,640]{1,0:T(8,128)(2,1)S(1)}, bf16[64,640]{1,0:T(8,128)(2,1)S(1)}) fusion(bf16[64,24576]{1,0:T(8,128)(2,1)} %bitcast.7), kind=kLoop, calls=%fused_computation.14 | loop fusion | bytes 327680 | tf_op jit(solution)/shard_map/slice | solution.py:401
  2.3 1.1 %fusion.4 = (bf16[192,640]{1,0:T(8,128)(2,1)S(1)}, bf16[192,640]{1,0:T(8,128)(2,1)S(1)}) fusion(bf16[192,24576]{1,0:T(8,128)(2,1)} %bitcast.4), kind=kLoop, calls=%fused_computation.13 | loop fusion | bytes 983040 | tf_op jit(solution)/shard_map/slice | solution.py:401
  3.5 4.9 %collective-permute-start = (bf16[272,640]{1,0:T(8,128)(2,1)S(1)}, bf16[272,640]{1,0:T(8,128)(2,1)S(1)}, u32[]{:S(2)}, u32[]{:S(2)}) collective-permute-start(bf16[272,640]{1,0:T(8,128)(2,1)S(1)} %pad_maximum_fusion), channel_id=1, source_target_pairs={{0,1},{1,2},{2,3},{3,4},{4,5},{5,6},{6,7},{7,8},{8,9},{9,10},{10,1... | collective-permute-start | bytes 1044488 | tf_op jit(solution)/shard_map/ppermute | solution.py:407
  8.4 1.3 %collective-permute-start.1 = (bf16[272,640]{1,0:T(8,128)(2,1)S(1)}, bf16[272,640]{1,0:T(8,128)(2,1)S(1)}, u32[]{:S(2)}, u32[]{:S(2)}) collective-permute-start(bf16[272,640]{1,0:T(8,128)(2,1)S(1)} %pad_maximum_fusion.1), channel_id=1, source_target_pairs={{1,0},{2,1},{3,2},{4,3},{5,4},{6,5},{7,6},{8,7},{9,8},{10,9},{11,1... | collective-permute-start | bytes 1044488 | tf_op jit(solution)/shard_map/ppermute | solution.py:408
  9.7 0.7 slice_add_fusion.1
  10.4 36.5 %interior.1 = (f32[64,24576]{1,0:T(8,128)}, f32[64,128]{1,0:T(8,128)}) custom-call(bf16[192,24576]{1,0:T(8,128)(2,1)} %bitcast.5, s32[1,24576]{1,0:T(1,128)} %bitcast.12, bf16[64,24576]{1,0:T(8,128)(2,1)} %bitcast.8), custom_call_target="tpu_custom_call" | custom-call | tf_op jit(solution)/shard_map/interior/pallas_call | solution.py:197
  47.0 0.0 copy-start
  47.0 0.0 collective-permute-done.1.high_ref
  47.0 0.7 pad_add_fusion.id_ref
  47.7 0.1 copy-done.1
  47.8 7.0 %ends.1 = (f32[64,24576]{1,0:T(8,128)}, f32[64,128]{1,0:T(8,128)}) custom-call(bf16[272,640]{1,0:T(8,128)(2,1)} %copy-done, bf16[272,640]{1,0:T(8,128)(2,1)} %copy-done.1, s32[1,3840]{1,0:T(1,128)} %pad_add_fusion.id_ref, f32[64,128]{1,0:T(8,128)} %get-tuple-element.8.sums_ref, bf16[192,24576]{1,0:T(8,128)(2,1)} %bitcast.6, ...), custom_call_target="tpu_custom_call", output_to_operand_aliasing={{0}: (6, {})} | custom-call | tf_op jit(solution)/shard_map/ends/pallas_call | solution.py:297
  54.8 3.8 %collective-permute-start.2 = (f32[64,128]{1,0:T(8,128)}, f32[64,128]{1,0:T(8,128)S(1)}, u32[]{:S(2)}, u32[]{:S(2)}) collective-permute-start(f32[64,128]{1,0:T(8,128)} %get-tuple-element.10), channel_id=1, source_target_pairs={{0,8},{8,0},{16,24},{24,16},{1,9},{9,1},{17,25},{25,17},{2,10},{10... | collective-permute-start | bytes 98312 | tf_op jit(solution)/shard_map/ppermute | solution.py:332
  58.7 1.1 %collective-permute-done.2 = f32[64,128]{1,0:T(8,128)S(1)} collective-permute-done((f32[64,128]{1,0:T(8,128)}, f32[64,128]{1,0:T(8,128)S(1)}, u32[]{:S(2)}, u32[]{:S(2)}) %collective-permute-start.2) | collective-permute-done | bytes 32800 | tf_op jit(solution)/shard_map/ppermute | solution.py:332
  59.7 0.8 add.31
  60.5 2.5 %collective-permute-start.3 = (f32[64,128]{1,0:T(8,128)S(1)}, f32[64,128]{1,0:T(8,128)S(1)}, u32[]{:S(2)}, u32[]{:S(2)}) collective-permute-start(f32[64,128]{1,0:T(8,128)S(1)} %add.31), channel_id=1, source_target_pairs={{0,16},{8,24},{16,0},{24,8},{1,17},{9,25},{17,1},{25,9},{2,18},{10... | collective-permute-start | bytes 98312 | tf_op jit(solution)/shard_map/ppermute | solution.py:332
  63.0 1.9 %collective-permute-done.3 = f32[64,128]{1,0:T(8,128)S(1)} collective-permute-done((f32[64,128]{1,0:T(8,128)S(1)}, f32[64,128]{1,0:T(8,128)S(1)}, u32[]{:S(2)}, u32[]{:S(2)}) %collective-permute-start.3) | collective-permute-done | bytes 32800 | tf_op jit(solution)/shard_map/ppermute | solution.py:332
  64.9 0.0 collective-permute-start.4
  64.9 3.9 %collective-permute-done.4 = f32[64,128]{1,0:T(8,128)S(1)} collective-permute-done((f32[64,128]{1,0:T(8,128)S(1)}, f32[64,128]{1,0:T(8,128)S(1)}, u32[]{:S(2)}, u32[]{:S(2)}) %collective-permute-start.4) | collective-permute-done | bytes 32800 | tf_op jit(solution)/shard_map/ppermute | solution.py:332
  68.8 3.9 %collective-permute-done.5 = f32[64,128]{1,0:T(8,128)S(1)} collective-permute-done((f32[64,128]{1,0:T(8,128)S(1)}, f32[64,128]{1,0:T(8,128)S(1)}, u32[]{:S(2)}, u32[]{:S(2)}) %collective-permute-start.5) | collective-permute-done | bytes 32800 | tf_op jit(solution)/shard_map/ppermute | solution.py:332
  72.7 0.7 collective-permute-start.6
  73.4 4.1 %collective-permute-done.6 = f32[64,128]{1,0:T(8,128)S(1)} collective-permute-done((f32[64,128]{1,0:T(8,128)S(1)}, f32[64,128]{1,0:T(8,128)S(1)}, u32[]{:S(2)}, u32[]{:S(2)}) %collective-permute-start.6) | collective-permute-done | bytes 32800 | tf_op jit(solution)/shard_map/ppermute | solution.py:332
  77.5 0.6 add.35.gram_ref
  78.2 10.5 %basis.1 = (f32[64,24576]{1,0:T(8,128)}, f32[64,64]{1,0:T(8,128)}) custom-call(f32[64,128]{1,0:T(8,128)} %add.35.gram_ref, f32[64,24576]{1,0:T(8,128)} %get-tuple-element.11.level_hbm), custom_call_target="tpu_custom_call" | custom-call | tf_op jit(solution)/shard_map/basis/pallas_call | solution.py:374
  (13 shorter events, 0.1 us)
Async XLA Ops:
  3.5 43.5 %collective-permute-start = (bf16[272,640]{1,0:T(8,128)(2,1)S(1)}, bf16[272,640]{1,0:T(8,128)(2,1)S(1)}, u32[]{:S(2)}, u32[]{:S(2)}) collective-permute-start(bf16[272,640]{1,0:T(8,128)(2,1)S(1)} %pad_maximum_fusion), channel_id=1, source_target_pairs={{0,1},{1,2},{2,3},{3,4},{4,5},{5,6},{6,7},{7,8},{8,9},{9,10},{10,1... | collective-permute-start | bytes 1044488 | tf_op jit(solution)/shard_map/ppermute | solution.py:407
  8.4 38.6 %collective-permute-start.1 = (bf16[272,640]{1,0:T(8,128)(2,1)S(1)}, bf16[272,640]{1,0:T(8,128)(2,1)S(1)}, u32[]{:S(2)}, u32[]{:S(2)}) collective-permute-start(bf16[272,640]{1,0:T(8,128)(2,1)S(1)} %pad_maximum_fusion.1), channel_id=1, source_target_pairs={{1,0},{2,1},{3,2},{4,3},{5,4},{6,5},{7,6},{8,7},{9,8},{10,9},{11,1... | collective-permute-start | bytes 1044488 | tf_op jit(solution)/shard_map/ppermute | solution.py:408
  47.0 0.8 copy-start
  47.0 0.8 copy-start.1
  54.8 4.9 %collective-permute-start.2 = (f32[64,128]{1,0:T(8,128)}, f32[64,128]{1,0:T(8,128)S(1)}, u32[]{:S(2)}, u32[]{:S(2)}) collective-permute-start(f32[64,128]{1,0:T(8,128)} %get-tuple-element.10), channel_id=1, source_target_pairs={{0,8},{8,0},{16,24},{24,16},{1,9},{9,1},{17,25},{25,17},{2,10},{10... | collective-permute-start | bytes 98312 | tf_op jit(solution)/shard_map/ppermute | solution.py:332
  60.5 4.4 %collective-permute-start.3 = (f32[64,128]{1,0:T(8,128)S(1)}, f32[64,128]{1,0:T(8,128)S(1)}, u32[]{:S(2)}, u32[]{:S(2)}) collective-permute-start(f32[64,128]{1,0:T(8,128)S(1)} %add.31), channel_id=1, source_target_pairs={{0,16},{8,24},{16,0},{24,8},{1,17},{9,25},{17,1},{25,9},{2,18},{10... | collective-permute-start | bytes 98312 | tf_op jit(solution)/shard_map/ppermute | solution.py:332
  64.9 3.9 %collective-permute-start.4 = (f32[64,128]{1,0:T(8,128)S(1)}, f32[64,128]{1,0:T(8,128)S(1)}, u32[]{:S(2)}, u32[]{:S(2)}) collective-permute-start(f32[64,128]{1,0:T(8,128)S(1)} %add.32), channel_id=1, source_target_pairs={{0,1},{1,0},{2,3},{3,2},{4,5},{5,4},{6,7},{7,6},{8,9},{9,8},{10,11... | collective-permute-start | bytes 98312 | tf_op jit(solution)/shard_map/ppermute | solution.py:332
  68.8 3.9 %collective-permute-start.5 = (f32[64,128]{1,0:T(8,128)S(1)}, f32[64,128]{1,0:T(8,128)S(1)}, u32[]{:S(2)}, u32[]{:S(2)}) collective-permute-start(f32[64,128]{1,0:T(8,128)S(1)} %add.33), channel_id=1, source_target_pairs={{0,2},{1,3},{2,0},{3,1},{4,6},{5,7},{6,4},{7,5},{8,10},{9,11},{10,... | collective-permute-start | bytes 98312 | tf_op jit(solution)/shard_map/ppermute | solution.py:332
  72.7 4.8 %collective-permute-start.6 = (f32[64,128]{1,0:T(8,128)S(1)}, f32[64,128]{1,0:T(8,128)S(1)}, u32[]{:S(2)}, u32[]{:S(2)}) collective-permute-start(f32[64,128]{1,0:T(8,128)S(1)} %add.34), channel_id=1, source_target_pairs={{0,4},{1,5},{2,6},{3,7},{4,0},{5,1},{6,2},{7,3},{8,12},{9,13},{10,... | collective-permute-start | bytes 98312 | tf_op jit(solution)/shard_map/ppermute | solution.py:332

commit v3 on v2

--- a/solution.py
+++ b/solution.py
@@ -10,10 +10,11 @@
 HALO = HALO_BLOCKS * BAND
 EMB = 192
 VECS = 64
-CHUNK_BLOCKS = 16
+CHUNK_BLOCKS = 32
 CHUNK = CHUNK_BLOCKS * BAND
 DEPTH = 256
 PENALTY = 64.0
+GROUP = 8
 EXPONENT = 4.328085122666891
 VMEM_BYTES = 62 << 20
 
@@ -50,34 +51,24 @@
 def affinity_pair(slot, block, carried, right, lhs_ref, rhs_ref, weight_ref, scale_ref):
     row = lax.broadcasted_iota(jnp.int32, (BAND, BAND), 0)
     col = lax.broadcasted_iota(jnp.int32, (BAND, BAND), 1)
-    here = slice(slot * BAND, (slot + 2) * BAND)
-    z = lax.dot_general(lhs_ref[:, here], rhs_ref[:, here], (((0,), (0,)), ((), ())), preferred_element_type=f32)
-    e = jnp.exp2(z * EXPONENT)
-    own0 = e[:BAND, :BAND].astype(bf16)
-    own1 = e[BAND:, BAND:].astype(bf16)
-    right0 = jnp.where(row <= col, e[BAND:, :BAND], 0.0).astype(bf16)
-    left1 = jnp.where(row >= col, e[:BAND, BAND:], 0.0).astype(bf16)
-    weight_ref[block, BAND : 2 * BAND, :] = own0
-    weight_ref[block, 2 * BAND :, :] = right0
-    weight_ref[block + 1, :BAND, :] = left1
-    weight_ref[block + 1, BAND : 2 * BAND, :] = own1
-    sum0 = jnp.sum(own0.astype(f32) + right0.astype(f32), axis=0, keepdims=True) + carried
-    scale_ref[:, columns(block * BAND, BAND)] = lax.rsqrt(sum0)
-    if not right:
-        return carried
-    z = lax.dot_general(
-        lhs_ref[:, (slot + 2) * BAND : (slot + 3) * BAND],
-        rhs_ref[:, (slot + 1) * BAND : (slot + 2) * BAND],
-        (((0,), (0,)), ((), ())),
-        preferred_element_type=f32,
-    )
-    right1 = jnp.where(row <= col, jnp.exp2(z * EXPONENT), 0.0).astype(bf16)
-    left2 = right1.T
-    weight_ref[block + 1, 2 * BAND :, :] = right1
-    weight_ref[block + 2, :BAND, :] = left2
-    sum1 = jnp.sum(own1.astype(f32) + left1.astype(f32) + right1.astype(f32), axis=0, keepdims=True)
-    scale_ref[:, columns(block * BAND + BAND, BAND)] = lax.rsqrt(sum1)
-    return jnp.sum(left2.astype(f32), axis=0, keepdims=True)
+    for i in range(2):
+        here = slice((slot + i) * BAND, (slot + i + 1) * BAND)
+        both = right or i == 0
+        there = slice((slot + i) * BAND, (slot + i + 1 + both) * BAND)
+        z = lax.dot_general(lhs_ref[:, there], rhs_ref[:, here], (((0,), (0,)), ((), ())), preferred_element_type=f32)
+        e = jnp.exp2(z * EXPONENT)
+        own = e[:BAND].astype(bf16)
+        weight_ref[block + i, BAND : 2 * BAND, :] = own
+        if not both:
+            return carried
+        after = jnp.where(row <= col, e[BAND:], 0.0).astype(bf16)
+        before = after.T
+        weight_ref[block + i, 2 * BAND :, :] = after
+        weight_ref[block + i + 1, :BAND, :] = before
+        degree = jnp.sum(own.astype(f32) + after.astype(f32), axis=0, keepdims=True) + carried
+        scale_ref[:, columns((block + i) * BAND, BAND)] = lax.rsqrt(degree)
+        carried = jnp.sum(before.astype(f32), axis=0, keepdims=True)
+    return carried
 
 
 def operators(lane, weight_ref, scale_ref, start_ref, pack_a, pack_b, level_a, level_b):
@@ -226,15 +217,49 @@
     )(emb, ids, start)
 
 
+def edges_kernel(emb_hbm, id_hbm, start_hbm, first_ref, last_ref, label_ref, sems):
+    rows = emb_hbm.shape[1]
+    copies = []
+    for side, (target, begin) in enumerate(((first_ref, 0), (last_ref, rows - HALO))):
+        there = slice(begin, begin + HALO)
+        copies += [
+            pltpu.make_async_copy(id_hbm.at[:, there], label_ref.at[side], sems.at[side, 0]),
+            pltpu.make_async_copy(emb_hbm.at[:, there], target.at[:EMB, :], sems.at[side, 1]),
+            pltpu.make_async_copy(start_hbm.at[:, there], target.at[EMB : EMB + VECS, :], sems.at[side, 2]),
+        ]
+    for copy in copies:
+        copy.start()
+    for side, target in enumerate((first_ref, last_ref)):
+        copies[3 * side].wait()
+        labels = jnp.broadcast_to(label_ref[side] + 1, (16, HALO)).astype(f32)
+        target[EMB + VECS :, :] = labels.astype(bf16)
+        copies[3 * side + 1].wait()
+        copies[3 * side + 2].wait()
+
+
+def edges(emb, ids, start):
+    whole = pl.BlockSpec(memory_space=pltpu.VMEM)
+    away = pl.BlockSpec(memory_space=pl.ANY)
+    return pl.pallas_call(
+        edges_kernel,
+        in_specs=[away, away, away],
+        out_specs=[whole, whole],
+        out_shape=[jax.ShapeDtypeStruct((EMB + VECS + 16, HALO), bf16)] * 2,
+        scratch_shapes=[pltpu.VMEM((2, 1, HALO), jnp.int32), pltpu.SemaphoreType.DMA((2, 3))],
+        compiler_params=pltpu.CompilerParams(vmem_limit_bytes=VMEM_BYTES),
+        name="edges",
+    )(emb, ids, start)
+
+
 INSIDE = 2 * HALO
 ENDS = 2 * (HALO + INSIDE)
 END_BLOCKS = ENDS // BAND
 
 
 def ends_kernel(
-    low_ref, high_ref, id_ref, sums_ref, emb_hbm, start_hbm, level_in,
+    low_ref, high_ref, sums_ref, id_hbm, emb_hbm, start_hbm, level_in,
     level_hbm, gram_ref,
-    emb_ref, lhs_ref, rhs_ref, weight_ref, scale_ref, start_ref, pack_a, pack_b, level_a, level_b, sems,
+    id_ref, emb_ref, lhs_ref, rhs_ref, weight_ref, scale_ref, start_ref, pack_a, pack_b, level_a, level_b, sems,
 ):
     rows = emb_hbm.shape[1]
     first = slice(0, INSIDE)
@@ -245,6 +270,8 @@
         pltpu.make_async_copy(source.at[:, there], target.at[:, here], sems.at[i])
         for i, (source, there, target, here) in enumerate(
             (
+                (id_hbm, first, id_ref, first_at),
+                (id_hbm, last, id_ref, last_at),
                 (emb_hbm, first, emb_ref, first_at),
                 (emb_hbm, last, emb_ref, last_at),
                 (start_hbm, first, start_ref, first_at),
@@ -258,11 +285,12 @@
         here = slice(begin, begin + HALO)
         emb_ref[:, here] = ref[:EMB, :]
         start_ref[:, here] = ref[EMB : EMB + VECS, :]
+        id_ref[:, here] = ref[EMB + VECS :, :].astype(f32)[:1].astype(jnp.int32) - 1
     for copy in copies:
         copy.wait()
     for j in range(ENDS // 256):
         here = slice(j * 256, j * 256 + 256)
-        prepare(emb_ref[:, here], id_ref[:, here], 2 * j, lhs_ref, rhs_ref)
+        prepare(emb_ref[:, here], id_ref[:, here] + 1, 2 * j, lhs_ref, rhs_ref)
     carried = jnp.zeros((1, BAND), f32)
     for i in range(END_BLOCKS // 2):
         carried = affinity_pair(
@@ -296,7 +324,7 @@
     away = pl.BlockSpec(memory_space=pl.ANY)
     return pl.pallas_call(
         ends_kernel,
-        in_specs=[whole, whole, whole, whole, away, away, away],
+        in_specs=[whole, whole, whole, away, away, away, away],
         out_specs=[away, whole],
         out_shape=[
             jax.ShapeDtypeStruct(level.shape, f32),
@@ -304,6 +332,7 @@
         ],
         input_output_aliases={6: 0},
         scratch_shapes=[
+            pltpu.VMEM((1, ENDS), jnp.int32),
             pltpu.VMEM((EMB, ENDS), bf16),
             pltpu.VMEM((DEPTH, ENDS), bf16),
             pltpu.VMEM((DEPTH, ENDS), bf16),
@@ -314,11 +343,11 @@
             pltpu.VMEM((VECS, ENDS), bf16),
             pltpu.VMEM((VECS, ENDS), f32),
             pltpu.VMEM((VECS, ENDS), f32),
-            pltpu.SemaphoreType.DMA((4,)),
+            pltpu.SemaphoreType.DMA((6,)),
         ],
         compiler_params=pltpu.CompilerParams(vmem_limit_bytes=VMEM_BYTES),
         name="ends",
-    )(low, high, ids, sums, emb, start, level)
+    )(low, high, sums, ids, emb, start, level)
 
 
 def total(x, axes):
@@ -344,11 +373,15 @@
         row = lax.broadcasted_iota(jnp.int32, (VECS, 2 * VECS), 0)
         col = lax.broadcasted_iota(jnp.int32, (VECS, 2 * VECS), 1)
         work = jnp.where(col < VECS, gram_ref[...], jnp.where(col == row + VECS, 1.0, 0.0))
-        for k in range(VECS - 1):
-            pivot = work[k : k + 1, :]
-            scaled = pivot / jnp.broadcast_to(pivot[:, k : k + 1], pivot.shape)
-            factor = jnp.where(row > k, jnp.broadcast_to(work[:, k : k + 1], work.shape), 0.0)
-            work = work - factor * scaled
+        for k in range(0, VECS, GROUP):
+            spread = [jnp.broadcast_to(work[:, j : j + 1], work.shape) for j in range(k, k + GROUP)]
+            pivots = [work[j : j + 1, :] for j in range(k, k + GROUP)]
+            for j in range(GROUP):
+                factor = jnp.where(row > k + j, spread[j] * (1.0 / spread[j][k + j : k + j + 1, :]), 0.0)
+                for m in range(j + 1, GROUP):
+                    spread[m] = spread[m] - factor * spread[m][k + j : k + j + 1, :]
+                    pivots[m] = pivots[m] - factor[k + m : k + m + 1, :] * pivots[j]
+                work = work - factor * pivots[j]
         diagonal = jnp.sum(jnp.where(row == col, work, 0.0), axis=1, keepdims=True)
         inverse = (work * lax.rsqrt(diagonal))[:, VECS:]
         image = gram_ref[:, VECS:]
@@ -369,7 +402,7 @@
 
 def orthonormal(sums, level):
     rows = level.shape[1]
-    width = 4 * CHUNK
+    width = 2 * CHUNK
     whole = pl.BlockSpec(memory_space=pltpu.VMEM)
     return pl.pallas_call(
         basis_kernel,
@@ -395,28 +428,13 @@
     rows = emb.shape[1]
     ids = stream_ids.reshape(1, rows)
 
-    def edge(begin):
-        here = slice(begin, begin + HALO)
-        labels = jnp.broadcast_to((ids[:, here] + 1).astype(bf16), (16, HALO))
-        return jnp.concatenate([emb[:, here], start[:, here], labels], axis=0)
-
+    first, last = edges(emb, ids, start)
     axes = ("ta", "au")
-    last = lax.axis_size(axes) - 1
-    up = [(i, i + 1) for i in range(last)]
-    down = [(i + 1, i) for i in range(last)]
-    low = lax.ppermute(edge(rows - HALO), axes, up)
-    high = lax.ppermute(edge(0), axes, down)
+    steps = range(lax.axis_size(axes) - 1)
+    low = lax.ppermute(last, axes, [(i, i + 1) for i in steps])
+    high = lax.ppermute(first, axes, [(i + 1, i) for i in steps])
     level, sums = interior(emb, ids, start)
-    labels = jnp.concatenate(
-        [
-            low[EMB + VECS : EMB + VECS + 1, :].astype(jnp.int32),
-            ids[:, :INSIDE] + 1,
-            ids[:, rows - INSIDE :] + 1,
-            high[EMB + VECS : EMB + VECS + 1, :].astype(jnp.int32),
-        ],
-        axis=1,
-    )
-    level, sums = ends(low, high, labels, sums, emb, start, level)
+    level, sums = ends(low, high, ids, sums, emb, start, level)
     basis, ritz = orthonormal(total(sums, axes), level)
     return basis.T, ritz
 

time: 89.5 us -> 85.1 us (0.951)
  other arithmetic: 3.62 us -> 1.4 us
  local copies, waits for them, and re-layouts: 2.16 us -> 0.82 us
    slice x2 -> x0, local copies, waits for them, and re-layouts: 2.05 us -> none  [edge(): return jnp.concatenate([emb[:, here], start[:, here], labels], axis=0)]
    pallas_call x1 -> x2, Pallas kernels: 7.01 us -> 8.96 us  [the longest x1 6.85 us: ends(): pl.pallas_call(ends_kernel, in_specs=[whole, whole, whole, away, away, aw...]
    pallas_call x1, Pallas kernels: 10.5 us -> 9.09 us  [orthonormal(): pl.pallas_call(basis_kernel, grid=(rows // width,), in_specs=[whole, pl.B...]
    pallas_call x1, Pallas kernels: 36.5 us -> 35.4 us  [interior(): pl.pallas_call(interior_kernel, grid=(rows // CHUNK,), in_specs=[pl.Block...]
  transfers between devices with their start and end apart: 7 -> 7, of which waited for: 5 -> 5; matrix products, arithmetic and copies ran while one was open for 1% -> 0% of each run, Pallas kernels for 41% -> 42%
where the time goes in v3:
time: 85.1 us; the launch traced here: 84.7 us
  Pallas kernels  53.5 us (63%)
  waiting for transfers between devices  14.9 us (18%)
  starting transfers between devices  13.2 us (16%)
  other arithmetic  1.4 us (2%)
  between operations  0.88 us (1%)
    pallas_call x1, Pallas kernels, interior(): pl.pallas_call(interior_kernel, grid=(rows // CHUNK,), in_specs=[pl.Block...  35.4 us
    ppermute x5, waiting for transfers between devices, total(): x = x + lax.ppermute(x, axis, [(i, i ^ stride) for i in range(size)])  14.9 us
    pallas_call x1, Pallas kernels, orthonormal(): pl.pallas_call(basis_kernel, grid=(rows // width,), in_specs=[whole, pl.B...  9.09 us
    ppermute x5, starting transfers between devices, total(): x = x + lax.ppermute(x, axis, [(i, i ^ stride) for i in range(size)])  7.04 us
    pallas_call x1, Pallas kernels, ends(): pl.pallas_call(ends_kernel, in_specs=[whole, whole, whole, away, away, aw...  6.85 us
    ppermute x1, starting transfers between devices, per_device(): low = lax.ppermute(last, axes, [(i, i + 1) for i in steps])  4.89 us
    pallas_call x1, Pallas kernels, edges(): pl.pallas_call(edges_kernel, in_specs=[away, away, away], out_specs=[whol...  2.1 us
  transfers between devices with their start and end apart: 7, of which 5 were waited for; matrix products, arithmetic and copies ran while one was open for 0% of the time, Pallas kernels for 42%

profile of v3, /device:TPU:0, one launch (start us, length us, event | category | flops | bytes accessed | tf_op | source)
XLA Modules:
  0.0 84.7 jit_solution(7424018678547370030)
XLA Ops:
  0.6 2.1 %edges.1 = (bf16[272,640]{1,0:T(8,128)(2,1)}, bf16[272,640]{1,0:T(8,128)(2,1)}) custom-call(bf16[192,24576]{1,0:T(8,128)(2,1)} %bitcast.4, s32[1,24576]{1,0:T(1,128)} %bitcast.10, bf16[64,24576]{1,0:T(8,128)(2,1)} %bitcast.7), custom_call_target="tpu_custom_call" | custom-call | tf_op jit(solution)/shard_map/edges/pallas_call | solution.py:243
  2.7 4.9 %collective-permute-start = (bf16[272,640]{1,0:T(8,128)(2,1)}, bf16[272,640]{1,0:T(8,128)(2,1)S(1)}, u32[]{:S(2)}, u32[]{:S(2)}) collective-permute-start(bf16[272,640]{1,0:T(8,128)(2,1)} %get-tuple-element.10), channel_id=1, source_target_pairs={{0,1},{1,2},{2,3},{3,4},{4,5},{5,6},{6,7},{7,8},{8,9},{9,10},{10,1... | collective-permute-start | bytes 1044488 | tf_op jit(solution)/shard_map/ppermute | solution.py:434
  7.6 1.3 %collective-permute-start.1 = (bf16[272,640]{1,0:T(8,128)(2,1)}, bf16[272,640]{1,0:T(8,128)(2,1)S(1)}, u32[]{:S(2)}, u32[]{:S(2)}) collective-permute-start(bf16[272,640]{1,0:T(8,128)(2,1)} %get-tuple-element.11), channel_id=1, source_target_pairs={{1,0},{2,1},{3,2},{4,3},{5,4},{6,5},{7,6},{8,7},{9,8},{10,9},{11,1... | collective-permute-start | bytes 1044488 | tf_op jit(solution)/shard_map/ppermute | solution.py:435
  8.9 35.4 %interior.1 = (f32[64,24576]{1,0:T(8,128)}, f32[64,128]{1,0:T(8,128)}) custom-call(bf16[192,24576]{1,0:T(8,128)(2,1)} %bitcast.5, s32[1,24576]{1,0:T(1,128)} %bitcast.11, bf16[64,24576]{1,0:T(8,128)(2,1)} %bitcast.8), custom_call_target="tpu_custom_call" | custom-call | tf_op jit(solution)/shard_map/interior/pallas_call | solution.py:188
  44.4 0.0 collective-permute-done.low_ref
  44.4 0.0 copy-start
  44.4 0.0 collective-permute-done.1.high_ref
  44.4 0.0 copy-start.1
  44.4 0.7 copy-done
  45.1 0.1 copy-done.1
  45.2 6.9 %ends.1 = (f32[64,24576]{1,0:T(8,128)}, f32[64,128]{1,0:T(8,128)}) custom-call(bf16[272,640]{1,0:T(8,128)(2,1)} %copy-done, bf16[272,640]{1,0:T(8,128)(2,1)} %copy-done.1, f32[64,128]{1,0:T(8,128)} %get-tuple-element.12.sums_ref, s32[1,24576]{1,0:T(1,128)} %bitcast.12, bf16[192,24576]{1,0:T(8,128)(2,1)} %bitcast.6, ...), custom_call_target="tpu_custom_call", output_to_operand_aliasing={{0}: (6, {})} | custom-call | tf_op jit(solution)/shard_map/ends/pallas_call | solution.py:325
  52.1 3.8 %collective-permute-start.2 = (f32[64,128]{1,0:T(8,128)}, f32[64,128]{1,0:T(8,128)S(1)}, u32[]{:S(2)}, u32[]{:S(2)}) collective-permute-start(f32[64,128]{1,0:T(8,128)} %get-tuple-element.14), channel_id=1, source_target_pairs={{0,8},{8,0},{16,24},{24,16},{1,9},{9,1},{17,25},{25,17},{2,10},{10... | collective-permute-start | bytes 98312 | tf_op jit(solution)/shard_map/ppermute | solution.py:361
  55.9 1.1 %collective-permute-done.2 = f32[64,128]{1,0:T(8,128)S(1)} collective-permute-done((f32[64,128]{1,0:T(8,128)}, f32[64,128]{1,0:T(8,128)S(1)}, u32[]{:S(2)}, u32[]{:S(2)}) %collective-permute-start.2) | collective-permute-done | bytes 32800 | tf_op jit(solution)/shard_map/ppermute | solution.py:361
  57.0 0.8 add.15
  57.8 2.5 %collective-permute-start.3 = (f32[64,128]{1,0:T(8,128)S(1)}, f32[64,128]{1,0:T(8,128)S(1)}, u32[]{:S(2)}, u32[]{:S(2)}) collective-permute-start(f32[64,128]{1,0:T(8,128)S(1)} %add.15), channel_id=1, source_target_pairs={{0,16},{8,24},{16,0},{24,8},{1,17},{9,25},{17,1},{25,9},{2,18},{10... | collective-permute-start | bytes 98312 | tf_op jit(solution)/shard_map/ppermute | solution.py:361
  60.3 1.9 %collective-permute-done.3 = f32[64,128]{1,0:T(8,128)S(1)} collective-permute-done((f32[64,128]{1,0:T(8,128)S(1)}, f32[64,128]{1,0:T(8,128)S(1)}, u32[]{:S(2)}, u32[]{:S(2)}) %collective-permute-start.3) | collective-permute-done | bytes 32800 | tf_op jit(solution)/shard_map/ppermute | solution.py:361
  62.2 0.0 collective-permute-start.4
  62.2 3.9 %collective-permute-done.4 = f32[64,128]{1,0:T(8,128)S(1)} collective-permute-done((f32[64,128]{1,0:T(8,128)S(1)}, f32[64,128]{1,0:T(8,128)S(1)}, u32[]{:S(2)}, u32[]{:S(2)}) %collective-permute-start.4) | collective-permute-done | bytes 32800 | tf_op jit(solution)/shard_map/ppermute | solution.py:361
  66.1 0.0 collective-permute-start.5
  66.1 3.9 %collective-permute-done.5 = f32[64,128]{1,0:T(8,128)S(1)} collective-permute-done((f32[64,128]{1,0:T(8,128)S(1)}, f32[64,128]{1,0:T(8,128)S(1)}, u32[]{:S(2)}, u32[]{:S(2)}) %collective-permute-start.5) | collective-permute-done | bytes 32800 | tf_op jit(solution)/shard_map/ppermute | solution.py:361
  70.0 0.7 collective-permute-start.6
  70.7 4.1 %collective-permute-done.6 = f32[64,128]{1,0:T(8,128)S(1)} collective-permute-done((f32[64,128]{1,0:T(8,128)S(1)}, f32[64,128]{1,0:T(8,128)S(1)}, u32[]{:S(2)}, u32[]{:S(2)}) %collective-permute-start.6) | collective-permute-done | bytes 32800 | tf_op jit(solution)/shard_map/ppermute | solution.py:361
  74.8 0.6 add.19.gram_ref
  75.4 9.1 %basis.1 = (f32[64,24576]{1,0:T(8,128)}, f32[64,64]{1,0:T(8,128)}) custom-call(f32[64,128]{1,0:T(8,128)} %add.19.gram_ref, f32[64,24576]{1,0:T(8,128)} %get-tuple-element.15.level_hbm), custom_call_target="tpu_custom_call" | custom-call | tf_op jit(solution)/shard_map/basis/pallas_call | solution.py:407
  (3 shorter events, 0.0 us)
Async XLA Ops:
  2.7 41.7 %collective-permute-start = (bf16[272,640]{1,0:T(8,128)(2,1)}, bf16[272,640]{1,0:T(8,128)(2,1)S(1)}, u32[]{:S(2)}, u32[]{:S(2)}) collective-permute-start(bf16[272,640]{1,0:T(8,128)(2,1)} %get-tuple-element.10), channel_id=1, source_target_pairs={{0,1},{1,2},{2,3},{3,4},{4,5},{5,6},{6,7},{7,8},{8,9},{9,10},{10,1... | collective-permute-start | bytes 1044488 | tf_op jit(solution)/shard_map/ppermute | solution.py:434
  7.6 36.8 %collective-permute-start.1 = (bf16[272,640]{1,0:T(8,128)(2,1)}, bf16[272,640]{1,0:T(8,128)(2,1)S(1)}, u32[]{:S(2)}, u32[]{:S(2)}) collective-permute-start(bf16[272,640]{1,0:T(8,128)(2,1)} %get-tuple-element.11), channel_id=1, source_target_pairs={{1,0},{2,1},{3,2},{4,3},{5,4},{6,5},{7,6},{8,7},{9,8},{10,9},{11,1... | collective-permute-start | bytes 1044488 | tf_op jit(solution)/shard_map/ppermute | solution.py:435
  44.4 0.7 copy-start
  44.4 0.8 copy-start.1
  52.1 4.9 %collective-permute-start.2 = (f32[64,128]{1,0:T(8,128)}, f32[64,128]{1,0:T(8,128)S(1)}, u32[]{:S(2)}, u32[]{:S(2)}) collective-permute-start(f32[64,128]{1,0:T(8,128)} %get-tuple-element.14), channel_id=1, source_target_pairs={{0,8},{8,0},{16,24},{24,16},{1,9},{9,1},{17,25},{25,17},{2,10},{10... | collective-permute-start | bytes 98312 | tf_op jit(solution)/shard_map/ppermute | solution.py:361
  57.8 4.4 %collective-permute-start.3 = (f32[64,128]{1,0:T(8,128)S(1)}, f32[64,128]{1,0:T(8,128)S(1)}, u32[]{:S(2)}, u32[]{:S(2)}) collective-permute-start(f32[64,128]{1,0:T(8,128)S(1)} %add.15), channel_id=1, source_target_pairs={{0,16},{8,24},{16,0},{24,8},{1,17},{9,25},{17,1},{25,9},{2,18},{10... | collective-permute-start | bytes 98312 | tf_op jit(solution)/shard_map/ppermute | solution.py:361
  62.2 3.9 %collective-permute-start.4 = (f32[64,128]{1,0:T(8,128)S(1)}, f32[64,128]{1,0:T(8,128)S(1)}, u32[]{:S(2)}, u32[]{:S(2)}) collective-permute-start(f32[64,128]{1,0:T(8,128)S(1)} %add.16), channel_id=1, source_target_pairs={{0,1},{1,0},{2,3},{3,2},{4,5},{5,4},{6,7},{7,6},{8,9},{9,8},{10,11... | collective-permute-start | bytes 98312 | tf_op jit(solution)/shard_map/ppermute | solution.py:361
  66.1 3.9 %collective-permute-start.5 = (f32[64,128]{1,0:T(8,128)S(1)}, f32[64,128]{1,0:T(8,128)S(1)}, u32[]{:S(2)}, u32[]{:S(2)}) collective-permute-start(f32[64,128]{1,0:T(8,128)S(1)} %add.17), channel_id=1, source_target_pairs={{0,2},{1,3},{2,0},{3,1},{4,6},{5,7},{6,4},{7,5},{8,10},{9,11},{10,... | collective-permute-start | bytes 98312 | tf_op jit(solution)/shard_map/ppermute | solution.py:361
  70.0 4.8 %collective-permute-start.6 = (f32[64,128]{1,0:T(8,128)S(1)}, f32[64,128]{1,0:T(8,128)S(1)}, u32[]{:S(2)}, u32[]{:S(2)}) collective-permute-start(f32[64,128]{1,0:T(8,128)S(1)} %add.18), channel_id=1, source_target_pairs={{0,4},{1,5},{2,6},{3,7},{4,0},{5,1},{6,2},{7,3},{8,12},{9,13},{10,... | collective-permute-start | bytes 98312 | tf_op jit(solution)/shard_map/ppermute | solution.py:361

commit v4 on v3

--- a/solution.py
+++ b/solution.py
@@ -15,6 +15,7 @@
 DEPTH = 256
 PENALTY = 64.0
 GROUP = 8
+GRAM_BLOCKS = 26
 EXPONENT = 4.328085122666891
 VMEM_BYTES = 62 << 20
 
@@ -23,6 +24,8 @@
 
 
 def columns(start, size):
+    if isinstance(start, int):
+        return slice(start, start + size)
     return pl.ds(pl.multiple_of(start, BAND), size)
 
 
@@ -115,23 +118,10 @@
     return jnp.concatenate([gram, image], axis=1)
 
 
-def loop(first, number, unroll, one):
-    def body(i, carry):
-        for u in range(unroll):
-            one(first + i * unroll + u)
-        return carry
-
-    lax.fori_loop(0, number // unroll, body, 0)
-
-
-def unrolled(number, most):
-    return max(u for u in range(1, most + 1) if number % u == 0)
-
-
 def interior_kernel(
     emb_ref, id_ref, chunk_ref,
     level_hbm, gram_ref,
-    lhs_ref, rhs_ref, weight_ref, scale_ref, carry_ref, start_ref, pack_a, pack_b, level_a, level_b, sum_ref, sems,
+    lhs_ref, rhs_ref, weight_ref, scale_ref, carry_ref, start_ref, pack_a, pack_b, level_a, level_b, sems,
 ):
     step = pl.program_id(0)
     count = pl.num_programs(0)
@@ -139,7 +129,6 @@
     @pl.when(step == 0)
     def _():
         carry_ref[...] = jnp.zeros_like(carry_ref)
-        sum_ref[...] = jnp.zeros_like(sum_ref)
         lhs_ref[:, :BAND] = jnp.zeros((DEPTH, BAND), bf16)
         rhs_ref[:, :BAND] = jnp.zeros((DEPTH, BAND), bf16)
 
@@ -161,24 +150,17 @@
         pack0, level1, level2, level3, products = operators(
             lambda b: b * BAND, weight_ref, scale_ref, start_ref, pack_a, pack_b, level_a, level_b
         )
-        number = own - 2
-        loop(2, number, unrolled(number, 100), pack0)
-        loop(2, number, unrolled(number, 100), level1)
-        loop(2, number, unrolled(number, 100), level2)
-        loop(2, number, unrolled(number, 100), level3)
+        for one in (pack0, level1, level2, level3):
+            for b in range(2, own):
+                one(b)
         inner = slice((HALO_BLOCKS + 1) * BAND, (own + 1 - HALO_BLOCKS) * BAND)
         outer = slice(HALO_BLOCKS * BAND, (own - HALO_BLOCKS) * BAND)
         out_copy = pltpu.make_async_copy(level_a.at[:, inner], level_hbm.at[:, outer], sems)
         out_copy.start()
-        number = own - 2 * HALO_BLOCKS
-        group = unrolled(number, 26)
-
-        def body(i, carry):
-            sum_ref[...] += products(HALO_BLOCKS + 1 + i * group, group)
-            return carry
-
-        lax.fori_loop(0, number // group, body, 0)
-        gram_ref[...] = combine(sum_ref[...])
+        sums = jnp.zeros((3 * VECS, 2 * VECS), f32)
+        for b in range(HALO_BLOCKS + 1, own + 1 - HALO_BLOCKS, GRAM_BLOCKS):
+            sums += products(b, min(GRAM_BLOCKS, own + 1 - HALO_BLOCKS - b))
+        gram_ref[...] = combine(sums)
         out_copy.wait()
 
 
@@ -209,7 +191,6 @@
             pltpu.VMEM((VECS, blocks * BAND), bf16),
             pltpu.VMEM((VECS, blocks * BAND), f32),
             pltpu.VMEM((VECS, blocks * BAND), f32),
-            pltpu.VMEM((3 * VECS, 2 * VECS), f32),
             pltpu.SemaphoreType.DMA,
         ],
         compiler_params=pltpu.CompilerParams(vmem_limit_bytes=VMEM_BYTES, dimension_semantics=("arbitrary",)),
@@ -217,7 +198,7 @@
     )(emb, ids, start)
 
 
-def edges_kernel(emb_hbm, id_hbm, start_hbm, first_ref, last_ref, label_ref, sems):
+def edges_kernel(emb_hbm, id_hbm, start_hbm, first_ref, last_ref, label_ref, row_ref, sems):
     rows = emb_hbm.shape[1]
     copies = []
     for side, (target, begin) in enumerate(((first_ref, 0), (last_ref, rows - HALO))):
@@ -229,23 +210,31 @@
         ]
     for copy in copies:
         copy.start()
+    rows = []
     for side, target in enumerate((first_ref, last_ref)):
         copies[3 * side].wait()
         labels = jnp.broadcast_to(label_ref[side] + 1, (16, HALO)).astype(f32)
-        target[EMB + VECS :, :] = labels.astype(bf16)
+        row_ref[side] = labels.astype(bf16)
+        rows.append(pltpu.make_async_copy(row_ref.at[side], target.at[EMB + VECS :, :], sems.at[side, 3]))
+        rows[side].start()
+    for side in range(2):
         copies[3 * side + 1].wait()
         copies[3 * side + 2].wait()
+        rows[side].wait()
 
 
 def edges(emb, ids, start):
-    whole = pl.BlockSpec(memory_space=pltpu.VMEM)
     away = pl.BlockSpec(memory_space=pl.ANY)
     return pl.pallas_call(
         edges_kernel,
         in_specs=[away, away, away],
-        out_specs=[whole, whole],
+        out_specs=[away, away],
         out_shape=[jax.ShapeDtypeStruct((EMB + VECS + 16, HALO), bf16)] * 2,
-        scratch_shapes=[pltpu.VMEM((2, 1, HALO), jnp.int32), pltpu.SemaphoreType.DMA((2, 3))],
+        scratch_shapes=[
+            pltpu.VMEM((2, 1, HALO), jnp.int32),
+            pltpu.VMEM((2, 16, HALO), bf16),
+            pltpu.SemaphoreType.DMA((2, 4)),
+        ],
         compiler_params=pltpu.CompilerParams(vmem_limit_bytes=VMEM_BYTES),
         name="edges",
     )(emb, ids, start)
@@ -286,7 +275,7 @@
         emb_ref[:, here] = ref[:EMB, :]
         start_ref[:, here] = ref[EMB : EMB + VECS, :]
         id_ref[:, here] = ref[EMB + VECS :, :].astype(f32)[:1].astype(jnp.int32) - 1
-    for copy in copies:
+    for copy in copies[:4]:
         copy.wait()
     for j in range(ENDS // 256):
         here = slice(j * 256, j * 256 + 256)
@@ -299,8 +288,11 @@
     pack0, level1, level2, level3, products = operators(
         lambda b: b * BAND, weight_ref, scale_ref, start_ref, pack_a, pack_b, level_a, level_b
     )
+    half = END_BLOCKS // 2
+    for copy in copies[4:]:
+        copy.wait()
     for margin, one in ((1, pack0), (2, level1), (3, level2), (4, level3)):
-        for b in range(margin, END_BLOCKS - margin):
+        for b in (*range(margin, half - margin), *range(half + margin, END_BLOCKS - margin)):
             one(b)
     outs = [
         pltpu.make_async_copy(level_a.at[:, here], level_hbm.at[:, there], sems.at[i])

time: 85.1 us -> 101 us (1.19)
  Pallas kernels: 53.5 us -> 69.3 us
    pallas_call x1, Pallas kernels: 2.1 us -> 21 us  [edges(): pl.pallas_call(edges_kernel, in_specs=[away, away, away], out_specs=[away...]
    pallas_call x1, Pallas kernels: 35.4 us -> 32.4 us  [interior(): pl.pallas_call(interior_kernel, grid=(rows // CHUNK,), in_specs=[pl.Block...]
  transfers between devices with their start and end apart: 7 -> 7, of which waited for: 5 -> 5; matrix products, arithmetic and copies ran while one was open for 0% -> 0% of each run, Pallas kernels for 42% -> 32%
where the time goes in v4:
time: 101 us
  Pallas kernels  69.3 us (69%)
  waiting for transfers between devices  14.9 us (15%)
  starting transfers between devices  13.2 us (13%)
  other arithmetic  1.4 us (1%)
    pallas_call x1, Pallas kernels, interior(): pl.pallas_call(interior_kernel, grid=(rows // CHUNK,), in_specs=[pl.Block...  32.4 us
    pallas_call x1, Pallas kernels, edges(): pl.pallas_call(edges_kernel, in_specs=[away, away, away], out_specs=[away...  21 us
    ppermute x5, waiting for transfers between devices, total(): x = x + lax.ppermute(x, axis, [(i, i ^ stride) for i in range(size)])  14.9 us
    pallas_call x1, Pallas kernels, orthonormal(): pl.pallas_call(basis_kernel, grid=(rows // width,), in_specs=[whole, pl.B...  9.09 us
    ppermute x5, starting transfers between devices, total(): x = x + lax.ppermute(x, axis, [(i, i ^ stride) for i in range(size)])  7.04 us
    pallas_call x1, Pallas kernels, ends(): pl.pallas_call(ends_kernel, in_specs=[whole, whole, whole, away, away, aw...  6.86 us
    ppermute x1, starting transfers between devices, per_device(): low = lax.ppermute(last, axes, [(i, i + 1) for i in steps])  4.89 us
  transfers between devices with their start and end apart: 7, of which 5 were waited for; matrix products, arithmetic and copies ran while one was open for 0% of the time, Pallas kernels for 32%

profile of v4, /device:TPU:0, one launch (start us, length us, event | category | flops | bytes accessed | tf_op | source)
XLA Modules:
  0.0 100.5 jit_solution(3344300537338664361)
XLA Ops:
  0.6 21.0 %edges.1 = (bf16[272,640]{1,0:T(8,128)(2,1)}, bf16[272,640]{1,0:T(8,128)(2,1)}) custom-call(bf16[192,24576]{1,0:T(8,128)(2,1)} %bitcast.4, s32[1,24576]{1,0:T(1,128)} %bitcast.10, bf16[64,24576]{1,0:T(8,128)(2,1)} %bitcast.7), custom_call_target="tpu_custom_call" | custom-call | tf_op jit(solution)/shard_map/edges/pallas_call | solution.py:228
  21.7 4.9 %collective-permute-start = (bf16[272,640]{1,0:T(8,128)(2,1)}, bf16[272,640]{1,0:T(8,128)(2,1)S(1)}, u32[]{:S(2)}, u32[]{:S(2)}) collective-permute-start(bf16[272,640]{1,0:T(8,128)(2,1)} %get-tuple-element.10), channel_id=1, source_target_pairs={{0,1},{1,2},{2,3},{3,4},{4,5},{5,6},{6,7},{7,8},{8,9},{9,10},{10,1... | collective-permute-start | bytes 1044488 | tf_op jit(solution)/shard_map/ppermute | solution.py:426
  26.6 1.3 %collective-permute-start.1 = (bf16[272,640]{1,0:T(8,128)(2,1)}, bf16[272,640]{1,0:T(8,128)(2,1)S(1)}, u32[]{:S(2)}, u32[]{:S(2)}) collective-permute-start(bf16[272,640]{1,0:T(8,128)(2,1)} %get-tuple-element.11), channel_id=1, source_target_pairs={{1,0},{2,1},{3,2},{4,3},{5,4},{6,5},{7,6},{8,7},{9,8},{10,9},{11,1... | collective-permute-start | bytes 1044488 | tf_op jit(solution)/shard_map/ppermute | solution.py:427
  27.9 32.4 %interior.1 = (f32[64,24576]{1,0:T(8,128)}, f32[64,128]{1,0:T(8,128)}) custom-call(bf16[192,24576]{1,0:T(8,128)(2,1)} %bitcast.5, s32[1,24576]{1,0:T(1,128)} %bitcast.11, bf16[64,24576]{1,0:T(8,128)(2,1)} %bitcast.8), custom_call_target="tpu_custom_call" | custom-call | tf_op jit(solution)/shard_map/interior/pallas_call | solution.py:170
  60.2 0.0 collective-permute-done.low_ref
  60.2 0.0 copy-start
  60.3 0.0 collective-permute-done.1.high_ref
  60.3 0.0 copy-start.1
  60.3 0.7 copy-done
  61.0 0.1 copy-done.1
  61.1 6.9 %ends.1 = (f32[64,24576]{1,0:T(8,128)}, f32[64,128]{1,0:T(8,128)}) custom-call(bf16[272,640]{1,0:T(8,128)(2,1)} %copy-done, bf16[272,640]{1,0:T(8,128)(2,1)} %copy-done.1, f32[64,128]{1,0:T(8,128)} %get-tuple-element.12.sums_ref, s32[1,24576]{1,0:T(1,128)} %bitcast.12, bf16[192,24576]{1,0:T(8,128)(2,1)} %bitcast.6, ...), custom_call_target="tpu_custom_call", output_to_operand_aliasing={{0}: (6, {})} | custom-call | tf_op jit(solution)/shard_map/ends/pallas_call | solution.py:317
  68.0 3.8 %collective-permute-start.2 = (f32[64,128]{1,0:T(8,128)}, f32[64,128]{1,0:T(8,128)S(1)}, u32[]{:S(2)}, u32[]{:S(2)}) collective-permute-start(f32[64,128]{1,0:T(8,128)} %get-tuple-element.14), channel_id=1, source_target_pairs={{0,8},{8,0},{16,24},{24,16},{1,9},{9,1},{17,25},{25,17},{2,10},{10... | collective-permute-start | bytes 98312 | tf_op jit(solution)/shard_map/ppermute | solution.py:353
  71.8 1.1 %collective-permute-done.2 = f32[64,128]{1,0:T(8,128)S(1)} collective-permute-done((f32[64,128]{1,0:T(8,128)}, f32[64,128]{1,0:T(8,128)S(1)}, u32[]{:S(2)}, u32[]{:S(2)}) %collective-permute-start.2) | collective-permute-done | bytes 32800 | tf_op jit(solution)/shard_map/ppermute | solution.py:353
  72.9 0.8 add.15
  73.6 2.5 %collective-permute-start.3 = (f32[64,128]{1,0:T(8,128)S(1)}, f32[64,128]{1,0:T(8,128)S(1)}, u32[]{:S(2)}, u32[]{:S(2)}) collective-permute-start(f32[64,128]{1,0:T(8,128)S(1)} %add.15), channel_id=1, source_target_pairs={{0,16},{8,24},{16,0},{24,8},{1,17},{9,25},{17,1},{25,9},{2,18},{10... | collective-permute-start | bytes 98312 | tf_op jit(solution)/shard_map/ppermute | solution.py:353
  76.1 1.9 %collective-permute-done.3 = f32[64,128]{1,0:T(8,128)S(1)} collective-permute-done((f32[64,128]{1,0:T(8,128)S(1)}, f32[64,128]{1,0:T(8,128)S(1)}, u32[]{:S(2)}, u32[]{:S(2)}) %collective-permute-start.3) | collective-permute-done | bytes 32800 | tf_op jit(solution)/shard_map/ppermute | solution.py:353
  78.0 0.0 collective-permute-start.4
  78.0 3.9 %collective-permute-done.4 = f32[64,128]{1,0:T(8,128)S(1)} collective-permute-done((f32[64,128]{1,0:T(8,128)S(1)}, f32[64,128]{1,0:T(8,128)S(1)}, u32[]{:S(2)}, u32[]{:S(2)}) %collective-permute-start.4) | collective-permute-done | bytes 32800 | tf_op jit(solution)/shard_map/ppermute | solution.py:353
  81.9 0.0 collective-permute-start.5
  81.9 3.9 %collective-permute-done.5 = f32[64,128]{1,0:T(8,128)S(1)} collective-permute-done((f32[64,128]{1,0:T(8,128)S(1)}, f32[64,128]{1,0:T(8,128)S(1)}, u32[]{:S(2)}, u32[]{:S(2)}) %collective-permute-start.5) | collective-permute-done | bytes 32800 | tf_op jit(solution)/shard_map/ppermute | solution.py:353
  85.9 0.7 collective-permute-start.6
  86.6 4.1 %collective-permute-done.6 = f32[64,128]{1,0:T(8,128)S(1)} collective-permute-done((f32[64,128]{1,0:T(8,128)S(1)}, f32[64,128]{1,0:T(8,128)S(1)}, u32[]{:S(2)}, u32[]{:S(2)}) %collective-permute-start.6) | collective-permute-done | bytes 32800 | tf_op jit(solution)/shard_map/ppermute | solution.py:353
  90.7 0.6 add.19.gram_ref
  91.3 9.1 %basis.1 = (f32[64,24576]{1,0:T(8,128)}, f32[64,64]{1,0:T(8,128)}) custom-call(f32[64,128]{1,0:T(8,128)} %add.19.gram_ref, f32[64,24576]{1,0:T(8,128)} %get-tuple-element.15.level_hbm), custom_call_target="tpu_custom_call" | custom-call | tf_op jit(solution)/shard_map/basis/pallas_call | solution.py:399
  (3 shorter events, 0.0 us)
Async XLA Ops:
  21.7 38.6 %collective-permute-start = (bf16[272,640]{1,0:T(8,128)(2,1)}, bf16[272,640]{1,0:T(8,128)(2,1)S(1)}, u32[]{:S(2)}, u32[]{:S(2)}) collective-permute-start(bf16[272,640]{1,0:T(8,128)(2,1)} %get-tuple-element.10), channel_id=1, source_target_pairs={{0,1},{1,2},{2,3},{3,4},{4,5},{5,6},{6,7},{7,8},{8,9},{9,10},{10,1... | collective-permute-start | bytes 1044488 | tf_op jit(solution)/shard_map/ppermute | solution.py:426
  26.6 33.7 %collective-permute-start.1 = (bf16[272,640]{1,0:T(8,128)(2,1)}, bf16[272,640]{1,0:T(8,128)(2,1)S(1)}, u32[]{:S(2)}, u32[]{:S(2)}) collective-permute-start(bf16[272,640]{1,0:T(8,128)(2,1)} %get-tuple-element.11), channel_id=1, source_target_pairs={{1,0},{2,1},{3,2},{4,3},{5,4},{6,5},{7,6},{8,7},{9,8},{10,9},{11,1... | collective-permute-start | bytes 1044488 | tf_op jit(solution)/shard_map/ppermute | solution.py:427
  60.2 0.7 copy-start
  60.3 0.8 copy-start.1
  68.0 4.9 %collective-permute-start.2 = (f32[64,128]{1,0:T(8,128)}, f32[64,128]{1,0:T(8,128)S(1)}, u32[]{:S(2)}, u32[]{:S(2)}) collective-permute-start(f32[64,128]{1,0:T(8,128)} %get-tuple-element.14), channel_id=1, source_target_pairs={{0,8},{8,0},{16,24},{24,16},{1,9},{9,1},{17,25},{25,17},{2,10},{10... | collective-permute-start | bytes 98312 | tf_op jit(solution)/shard_map/ppermute | solution.py:353
  73.6 4.4 %collective-permute-start.3 = (f32[64,128]{1,0:T(8,128)S(1)}, f32[64,128]{1,0:T(8,128)S(1)}, u32[]{:S(2)}, u32[]{:S(2)}) collective-permute-start(f32[64,128]{1,0:T(8,128)S(1)} %add.15), channel_id=1, source_target_pairs={{0,16},{8,24},{16,0},{24,8},{1,17},{9,25},{17,1},{25,9},{2,18},{10... | collective-permute-start | bytes 98312 | tf_op jit(solution)/shard_map/ppermute | solution.py:353
  78.0 3.9 %collective-permute-start.4 = (f32[64,128]{1,0:T(8,128)S(1)}, f32[64,128]{1,0:T(8,128)S(1)}, u32[]{:S(2)}, u32[]{:S(2)}) collective-permute-start(f32[64,128]{1,0:T(8,128)S(1)} %add.16), channel_id=1, source_target_pairs={{0,1},{1,0},{2,3},{3,2},{4,5},{5,4},{6,7},{7,6},{8,9},{9,8},{10,11... | collective-permute-start | bytes 98312 | tf_op jit(solution)/shard_map/ppermute | solution.py:353
  81.9 3.9 %collective-permute-start.5 = (f32[64,128]{1,0:T(8,128)S(1)}, f32[64,128]{1,0:T(8,128)S(1)}, u32[]{:S(2)}, u32[]{:S(2)}) collective-permute-start(f32[64,128]{1,0:T(8,128)S(1)} %add.17), channel_id=1, source_target_pairs={{0,2},{1,3},{2,0},{3,1},{4,6},{5,7},{6,4},{7,5},{8,10},{9,11},{10,... | collective-permute-start | bytes 98312 | tf_op jit(solution)/shard_map/ppermute | solution.py:353
  85.9 4.8 %collective-permute-start.6 = (f32[64,128]{1,0:T(8,128)S(1)}, f32[64,128]{1,0:T(8,128)S(1)}, u32[]{:S(2)}, u32[]{:S(2)}) collective-permute-start(f32[64,128]{1,0:T(8,128)S(1)} %add.18), channel_id=1, source_target_pairs={{0,4},{1,5},{2,6},{3,7},{4,0},{5,1},{6,2},{7,3},{8,12},{9,13},{10,... | collective-permute-start | bytes 98312 | tf_op jit(solution)/shard_map/ppermute | solution.py:353

commit v5 on v4

--- a/solution.py
+++ b/solution.py
@@ -198,7 +198,7 @@
     )(emb, ids, start)
 
 
-def edges_kernel(emb_hbm, id_hbm, start_hbm, first_ref, last_ref, label_ref, row_ref, sems):
+def edges_kernel(emb_hbm, id_hbm, start_hbm, first_ref, last_ref, label_ref, sems):
     rows = emb_hbm.shape[1]
     copies = []
     for side, (target, begin) in enumerate(((first_ref, 0), (last_ref, rows - HALO))):
@@ -210,31 +210,23 @@
         ]
     for copy in copies:
         copy.start()
-    rows = []
     for side, target in enumerate((first_ref, last_ref)):
         copies[3 * side].wait()
         labels = jnp.broadcast_to(label_ref[side] + 1, (16, HALO)).astype(f32)
-        row_ref[side] = labels.astype(bf16)
-        rows.append(pltpu.make_async_copy(row_ref.at[side], target.at[EMB + VECS :, :], sems.at[side, 3]))
-        rows[side].start()
-    for side in range(2):
+        target[EMB + VECS :, :] = labels.astype(bf16)
         copies[3 * side + 1].wait()
         copies[3 * side + 2].wait()
-        rows[side].wait()
 
 
 def edges(emb, ids, start):
+    whole = pl.BlockSpec(memory_space=pltpu.VMEM)
     away = pl.BlockSpec(memory_space=pl.ANY)
     return pl.pallas_call(
         edges_kernel,
         in_specs=[away, away, away],
-        out_specs=[away, away],
+        out_specs=[whole, whole],
         out_shape=[jax.ShapeDtypeStruct((EMB + VECS + 16, HALO), bf16)] * 2,
-        scratch_shapes=[
-            pltpu.VMEM((2, 1, HALO), jnp.int32),
-            pltpu.VMEM((2, 16, HALO), bf16),
-            pltpu.SemaphoreType.DMA((2, 4)),
-        ],
+        scratch_shapes=[pltpu.VMEM((2, 1, HALO), jnp.int32), pltpu.SemaphoreType.DMA((2, 3))],
         compiler_params=pltpu.CompilerParams(vmem_limit_bytes=VMEM_BYTES),
         name="edges",
     )(emb, ids, start)

time: 101 us -> 82 us (0.81)
  Pallas kernels: 69.3 us -> 50.4 us
    pallas_call x1, Pallas kernels: 21 us -> 2.1 us  [edges(): pl.pallas_call(edges_kernel, in_specs=[away, away, away], out_specs=[whol...]
  transfers between devices with their start and end apart: 7 -> 7, of which waited for: 5 -> 5; matrix products, arithmetic and copies ran while one was open for 0% -> 0% of each run, Pallas kernels for 32% -> 40%
where the time goes in v5:
time: 82 us; the launch traced here: 81.6 us
  Pallas kernels  50.4 us (61%)
  waiting for transfers between devices  14.9 us (18%)
  starting transfers between devices  13.2 us (16%)
  other arithmetic  1.4 us (2%)
  between operations  0.88 us (1%)
    pallas_call x1, Pallas kernels, interior(): pl.pallas_call(interior_kernel, grid=(rows // CHUNK,), in_specs=[pl.Block...  32.4 us
    ppermute x5, waiting for transfers between devices, total(): x = x + lax.ppermute(x, axis, [(i, i ^ stride) for i in range(size)])  14.9 us
    pallas_call x1, Pallas kernels, orthonormal(): pl.pallas_call(basis_kernel, grid=(rows // width,), in_specs=[whole, pl.B...  9.09 us
    ppermute x5, starting transfers between devices, total(): x = x + lax.ppermute(x, axis, [(i, i ^ stride) for i in range(size)])  7.03 us
    pallas_call x1, Pallas kernels, ends(): pl.pallas_call(ends_kernel, in_specs=[whole, whole, whole, away, away, aw...  6.86 us
    ppermute x1, starting transfers between devices, per_device(): low = lax.ppermute(last, axes, [(i, i + 1) for i in steps])  4.89 us
    pallas_call x1, Pallas kernels, edges(): pl.pallas_call(edges_kernel, in_specs=[away, away, away], out_specs=[whol...  2.1 us
  transfers between devices with their start and end apart: 7, of which 5 were waited for; matrix products, arithmetic and copies ran while one was open for 0% of the time, Pallas kernels for 40%

profile of v5, /device:TPU:0, one launch (start us, length us, event | category | flops | bytes accessed | tf_op | source)
XLA Modules:
  0.0 81.6 jit_solution(15491060231004151539)
XLA Ops:
  0.6 2.1 %edges.1 = (bf16[272,640]{1,0:T(8,128)(2,1)}, bf16[272,640]{1,0:T(8,128)(2,1)}) custom-call(bf16[192,24576]{1,0:T(8,128)(2,1)} %bitcast.4, s32[1,24576]{1,0:T(1,128)} %bitcast.10, bf16[64,24576]{1,0:T(8,128)(2,1)} %bitcast.7), custom_call_target="tpu_custom_call" | custom-call | tf_op jit(solution)/shard_map/edges/pallas_call | solution.py:224
  2.7 4.9 %collective-permute-start = (bf16[272,640]{1,0:T(8,128)(2,1)}, bf16[272,640]{1,0:T(8,128)(2,1)S(1)}, u32[]{:S(2)}, u32[]{:S(2)}) collective-permute-start(bf16[272,640]{1,0:T(8,128)(2,1)} %get-tuple-element.10), channel_id=1, source_target_pairs={{0,1},{1,2},{2,3},{3,4},{4,5},{5,6},{6,7},{7,8},{8,9},{9,10},{10,1... | collective-permute-start | bytes 1044488 | tf_op jit(solution)/shard_map/ppermute | solution.py:418
  7.6 1.3 %collective-permute-start.1 = (bf16[272,640]{1,0:T(8,128)(2,1)}, bf16[272,640]{1,0:T(8,128)(2,1)S(1)}, u32[]{:S(2)}, u32[]{:S(2)}) collective-permute-start(bf16[272,640]{1,0:T(8,128)(2,1)} %get-tuple-element.11), channel_id=1, source_target_pairs={{1,0},{2,1},{3,2},{4,3},{5,4},{6,5},{7,6},{8,7},{9,8},{10,9},{11,1... | collective-permute-start | bytes 1044488 | tf_op jit(solution)/shard_map/ppermute | solution.py:419
  8.9 32.4 %interior.1 = (f32[64,24576]{1,0:T(8,128)}, f32[64,128]{1,0:T(8,128)}) custom-call(bf16[192,24576]{1,0:T(8,128)(2,1)} %bitcast.5, s32[1,24576]{1,0:T(1,128)} %bitcast.11, bf16[64,24576]{1,0:T(8,128)(2,1)} %bitcast.8), custom_call_target="tpu_custom_call" | custom-call | tf_op jit(solution)/shard_map/interior/pallas_call | solution.py:170
  41.3 0.0 collective-permute-done.low_ref
  41.3 0.0 copy-start
  41.3 0.0 collective-permute-done.1.high_ref
  41.3 0.0 copy-start.1
  41.4 0.7 copy-done
  42.1 0.1 copy-done.1
  42.2 6.9 %ends.1 = (f32[64,24576]{1,0:T(8,128)}, f32[64,128]{1,0:T(8,128)}) custom-call(bf16[272,640]{1,0:T(8,128)(2,1)} %copy-done, bf16[272,640]{1,0:T(8,128)(2,1)} %copy-done.1, f32[64,128]{1,0:T(8,128)} %get-tuple-element.12.sums_ref, s32[1,24576]{1,0:T(1,128)} %bitcast.12, bf16[192,24576]{1,0:T(8,128)(2,1)} %bitcast.6, ...), custom_call_target="tpu_custom_call", output_to_operand_aliasing={{0}: (6, {})} | custom-call | tf_op jit(solution)/shard_map/ends/pallas_call | solution.py:309
  49.0 3.8 %collective-permute-start.2 = (f32[64,128]{1,0:T(8,128)}, f32[64,128]{1,0:T(8,128)S(1)}, u32[]{:S(2)}, u32[]{:S(2)}) collective-permute-start(f32[64,128]{1,0:T(8,128)} %get-tuple-element.14), channel_id=1, source_target_pairs={{0,8},{8,0},{16,24},{24,16},{1,9},{9,1},{17,25},{25,17},{2,10},{10... | collective-permute-start | bytes 98312 | tf_op jit(solution)/shard_map/ppermute | solution.py:345
  52.9 1.1 %collective-permute-done.2 = f32[64,128]{1,0:T(8,128)S(1)} collective-permute-done((f32[64,128]{1,0:T(8,128)}, f32[64,128]{1,0:T(8,128)S(1)}, u32[]{:S(2)}, u32[]{:S(2)}) %collective-permute-start.2) | collective-permute-done | bytes 32800 | tf_op jit(solution)/shard_map/ppermute | solution.py:345
  53.9 0.8 add.15
  54.7 2.5 %collective-permute-start.3 = (f32[64,128]{1,0:T(8,128)S(1)}, f32[64,128]{1,0:T(8,128)S(1)}, u32[]{:S(2)}, u32[]{:S(2)}) collective-permute-start(f32[64,128]{1,0:T(8,128)S(1)} %add.15), channel_id=1, source_target_pairs={{0,16},{8,24},{16,0},{24,8},{1,17},{9,25},{17,1},{25,9},{2,18},{10... | collective-permute-start | bytes 98312 | tf_op jit(solution)/shard_map/ppermute | solution.py:345
  57.2 1.9 %collective-permute-done.3 = f32[64,128]{1,0:T(8,128)S(1)} collective-permute-done((f32[64,128]{1,0:T(8,128)S(1)}, f32[64,128]{1,0:T(8,128)S(1)}, u32[]{:S(2)}, u32[]{:S(2)}) %collective-permute-start.3) | collective-permute-done | bytes 32800 | tf_op jit(solution)/shard_map/ppermute | solution.py:345
  59.1 0.0 collective-permute-start.4
  59.1 3.9 %collective-permute-done.4 = f32[64,128]{1,0:T(8,128)S(1)} collective-permute-done((f32[64,128]{1,0:T(8,128)S(1)}, f32[64,128]{1,0:T(8,128)S(1)}, u32[]{:S(2)}, u32[]{:S(2)}) %collective-permute-start.4) | collective-permute-done | bytes 32800 | tf_op jit(solution)/shard_map/ppermute | solution.py:345
  63.0 0.0 collective-permute-start.5
  63.0 3.9 %collective-permute-done.5 = f32[64,128]{1,0:T(8,128)S(1)} collective-permute-done((f32[64,128]{1,0:T(8,128)S(1)}, f32[64,128]{1,0:T(8,128)S(1)}, u32[]{:S(2)}, u32[]{:S(2)}) %collective-permute-start.5) | collective-permute-done | bytes 32800 | tf_op jit(solution)/shard_map/ppermute | solution.py:345
  66.9 0.7 collective-permute-start.6
  67.6 4.1 %collective-permute-done.6 = f32[64,128]{1,0:T(8,128)S(1)} collective-permute-done((f32[64,128]{1,0:T(8,128)S(1)}, f32[64,128]{1,0:T(8,128)S(1)}, u32[]{:S(2)}, u32[]{:S(2)}) %collective-permute-start.6) | collective-permute-done | bytes 32800 | tf_op jit(solution)/shard_map/ppermute | solution.py:345
  71.7 0.6 add.19.gram_ref
  72.4 9.1 %basis.1 = (f32[64,24576]{1,0:T(8,128)}, f32[64,64]{1,0:T(8,128)}) custom-call(f32[64,128]{1,0:T(8,128)} %add.19.gram_ref, f32[64,24576]{1,0:T(8,128)} %get-tuple-element.15.level_hbm), custom_call_target="tpu_custom_call" | custom-call | tf_op jit(solution)/shard_map/basis/pallas_call | solution.py:391
  (3 shorter events, 0.0 us)
Async XLA Ops:
  2.7 38.6 %collective-permute-start = (bf16[272,640]{1,0:T(8,128)(2,1)}, bf16[272,640]{1,0:T(8,128)(2,1)S(1)}, u32[]{:S(2)}, u32[]{:S(2)}) collective-permute-start(bf16[272,640]{1,0:T(8,128)(2,1)} %get-tuple-element.10), channel_id=1, source_target_pairs={{0,1},{1,2},{2,3},{3,4},{4,5},{5,6},{6,7},{7,8},{8,9},{9,10},{10,1... | collective-permute-start | bytes 1044488 | tf_op jit(solution)/shard_map/ppermute | solution.py:418
  7.6 33.7 %collective-permute-start.1 = (bf16[272,640]{1,0:T(8,128)(2,1)}, bf16[272,640]{1,0:T(8,128)(2,1)S(1)}, u32[]{:S(2)}, u32[]{:S(2)}) collective-permute-start(bf16[272,640]{1,0:T(8,128)(2,1)} %get-tuple-element.11), channel_id=1, source_target_pairs={{1,0},{2,1},{3,2},{4,3},{5,4},{6,5},{7,6},{8,7},{9,8},{10,9},{11,1... | collective-permute-start | bytes 1044488 | tf_op jit(solution)/shard_map/ppermute | solution.py:419
  41.3 0.7 copy-start
  41.3 0.8 %copy-start.1 = (bf16[272,640]{1,0:T(8,128)(2,1)}, bf16[272,640]{1,0:T(8,128)(2,1)S(1)}, u32[]{:S(2)}) copy-start(bf16[272,640]{1,0:T(8,128)(2,1)S(1)} %collective-permute-done.1.high_ref) | copy-start | bytes 1044484
  49.0 4.9 %collective-permute-start.2 = (f32[64,128]{1,0:T(8,128)}, f32[64,128]{1,0:T(8,128)S(1)}, u32[]{:S(2)}, u32[]{:S(2)}) collective-permute-start(f32[64,128]{1,0:T(8,128)} %get-tuple-element.14), channel_id=1, source_target_pairs={{0,8},{8,0},{16,24},{24,16},{1,9},{9,1},{17,25},{25,17},{2,10},{10... | collective-permute-start | bytes 98312 | tf_op jit(solution)/shard_map/ppermute | solution.py:345
  54.7 4.4 %collective-permute-start.3 = (f32[64,128]{1,0:T(8,128)S(1)}, f32[64,128]{1,0:T(8,128)S(1)}, u32[]{:S(2)}, u32[]{:S(2)}) collective-permute-start(f32[64,128]{1,0:T(8,128)S(1)} %add.15), channel_id=1, source_target_pairs={{0,16},{8,24},{16,0},{24,8},{1,17},{9,25},{17,1},{25,9},{2,18},{10... | collective-permute-start | bytes 98312 | tf_op jit(solution)/shard_map/ppermute | solution.py:345
  59.1 3.9 %collective-permute-start.4 = (f32[64,128]{1,0:T(8,128)S(1)}, f32[64,128]{1,0:T(8,128)S(1)}, u32[]{:S(2)}, u32[]{:S(2)}) collective-permute-start(f32[64,128]{1,0:T(8,128)S(1)} %add.16), channel_id=1, source_target_pairs={{0,1},{1,0},{2,3},{3,2},{4,5},{5,4},{6,7},{7,6},{8,9},{9,8},{10,11... | collective-permute-start | bytes 98312 | tf_op jit(solution)/shard_map/ppermute | solution.py:345
  63.0 3.9 %collective-permute-start.5 = (f32[64,128]{1,0:T(8,128)S(1)}, f32[64,128]{1,0:T(8,128)S(1)}, u32[]{:S(2)}, u32[]{:S(2)}) collective-permute-start(f32[64,128]{1,0:T(8,128)S(1)} %add.17), channel_id=1, source_target_pairs={{0,2},{1,3},{2,0},{3,1},{4,6},{5,7},{6,4},{7,5},{8,10},{9,11},{10,... | collective-permute-start | bytes 98312 | tf_op jit(solution)/shard_map/ppermute | solution.py:345
  66.9 4.8 %collective-permute-start.6 = (f32[64,128]{1,0:T(8,128)S(1)}, f32[64,128]{1,0:T(8,128)S(1)}, u32[]{:S(2)}, u32[]{:S(2)}) collective-permute-start(f32[64,128]{1,0:T(8,128)S(1)} %add.18), channel_id=1, source_target_pairs={{0,4},{1,5},{2,6},{3,7},{4,0},{5,1},{6,2},{7,3},{8,12},{9,13},{10,... | collective-permute-start | bytes 98312 | tf_op jit(solution)/shard_map/ppermute | solution.py:345

commit v6 on v5

--- a/solution.py
+++ b/solution.py
@@ -347,13 +347,18 @@
     return x
 
 
-def basis_kernel(gram_ref, level_hbm, basis_ref, ritz_ref, inverse_ref, level_ref, sem):
+def basis_kernel(gram_ref, level_hbm, basis_ref, ritz_ref, inverse_ref, level_ref, sems):
+    step = pl.program_id(0)
     width = basis_ref.shape[1]
 
-    @pl.when(pl.program_id(0) == 0)
+    def fetch(i):
+        here = columns(i * width, width)
+        return pltpu.make_async_copy(level_hbm.at[:, here], level_ref.at[:, here], sems.at[i])
+
+    @pl.when(step == 0)
     def _():
-        copy = pltpu.make_async_copy(level_hbm, level_ref, sem)
-        copy.start()
+        for i in range(level_ref.shape[1] // width):
+            fetch(i).start()
         row = lax.broadcasted_iota(jnp.int32, (VECS, 2 * VECS), 0)
         col = lax.broadcasted_iota(jnp.int32, (VECS, 2 * VECS), 1)
         work = jnp.where(col < VECS, gram_ref[...], jnp.where(col == row + VECS, 1.0, 0.0))
@@ -376,9 +381,9 @@
         )
         high, low = split(inverse)
         inverse_ref[...] = jnp.concatenate([high, high, low], axis=1)
-        copy.wait()
-
-    high, low = split(level_ref[:, columns(pl.program_id(0) * width, width)])
+
+    fetch(step).wait()
+    high, low = split(level_ref[:, columns(step * width, width)])
     basis_ref[...] = jnp.dot(
         inverse_ref[...], jnp.concatenate([high, low, high], axis=0), preferred_element_type=f32
     )
@@ -400,7 +405,7 @@
         scratch_shapes=[
             pltpu.VMEM((VECS, 3 * VECS), bf16),
             pltpu.VMEM((VECS, rows), f32),
-            pltpu.SemaphoreType.DMA,
+            pltpu.SemaphoreType.DMA((rows // width,)),
         ],
         compiler_params=pltpu.CompilerParams(vmem_limit_bytes=VMEM_BYTES),
         name="basis",

time: 82 us -> 80.8 us (0.985)
  Pallas kernels: 50.4 us -> 49.3 us
    pallas_call x1, Pallas kernels: 9.09 us -> 7.94 us  [orthonormal(): pl.pallas_call(basis_kernel, grid=(rows // width,), in_specs=[whole, pl.B...]
where the time goes in v6:
time: 80.8 us; the launch traced here: 80.5 us
  Pallas kernels  49.3 us (61%)
  waiting for transfers between devices  14.9 us (18%)
  starting transfers between devices  13.2 us (16%)
  other arithmetic  1.4 us (2%)
  between operations  0.88 us (1%)
  local copies, waits for them, and re-layouts  0.82 us (1%)
    pallas_call x1, Pallas kernels, interior(): pl.pallas_call(interior_kernel, grid=(rows // CHUNK,), in_specs=[pl.Block...  32.4 us
    ppermute x5, waiting for transfers between devices, total(): x = x + lax.ppermute(x, axis, [(i, i ^ stride) for i in range(size)])  14.9 us
    pallas_call x1, Pallas kernels, orthonormal(): pl.pallas_call(basis_kernel, grid=(rows // width,), in_specs=[whole, pl.B...  7.94 us
    ppermute x5, starting transfers between devices, total(): x = x + lax.ppermute(x, axis, [(i, i ^ stride) for i in range(size)])  7.03 us
    pallas_call x1, Pallas kernels, ends(): pl.pallas_call(ends_kernel, in_specs=[whole, whole, whole, away, away, aw...  6.86 us
    ppermute x1, starting transfers between devices, per_device(): low = lax.ppermute(last, axes, [(i, i + 1) for i in steps])  4.89 us
    pallas_call x1, Pallas kernels, edges(): pl.pallas_call(edges_kernel, in_specs=[away, away, away], out_specs=[whol...  2.1 us
  transfers between devices with their start and end apart: 7, of which 5 were waited for; matrix products, arithmetic and copies ran while one was open for 0% of the time, Pallas kernels for 40%

profile of v6, /device:TPU:0, one launch (start us, length us, event | category | flops | bytes accessed | tf_op | source)
XLA Modules:
  0.0 80.5 jit_solution(2522228132974263061)
XLA Ops:
  0.6 2.1 %edges.1 = (bf16[272,640]{1,0:T(8,128)(2,1)}, bf16[272,640]{1,0:T(8,128)(2,1)}) custom-call(bf16[192,24576]{1,0:T(8,128)(2,1)} %bitcast.4, s32[1,24576]{1,0:T(1,128)} %bitcast.10, bf16[64,24576]{1,0:T(8,128)(2,1)} %bitcast.7), custom_call_target="tpu_custom_call" | custom-call | tf_op jit(solution)/shard_map/edges/pallas_call | solution.py:224
  2.7 4.9 %collective-permute-start = (bf16[272,640]{1,0:T(8,128)(2,1)}, bf16[272,640]{1,0:T(8,128)(2,1)S(1)}, u32[]{:S(2)}, u32[]{:S(2)}) collective-permute-start(bf16[272,640]{1,0:T(8,128)(2,1)} %get-tuple-element.10), channel_id=1, source_target_pairs={{0,1},{1,2},{2,3},{3,4},{4,5},{5,6},{6,7},{7,8},{8,9},{9,10},{10,1... | collective-permute-start | bytes 1044488 | tf_op jit(solution)/shard_map/ppermute | solution.py:423
  7.6 1.3 %collective-permute-start.1 = (bf16[272,640]{1,0:T(8,128)(2,1)}, bf16[272,640]{1,0:T(8,128)(2,1)S(1)}, u32[]{:S(2)}, u32[]{:S(2)}) collective-permute-start(bf16[272,640]{1,0:T(8,128)(2,1)} %get-tuple-element.11), channel_id=1, source_target_pairs={{1,0},{2,1},{3,2},{4,3},{5,4},{6,5},{7,6},{8,7},{9,8},{10,9},{11,1... | collective-permute-start | bytes 1044488 | tf_op jit(solution)/shard_map/ppermute | solution.py:424
  8.9 32.4 %interior.1 = (f32[64,24576]{1,0:T(8,128)}, f32[64,128]{1,0:T(8,128)}) custom-call(bf16[192,24576]{1,0:T(8,128)(2,1)} %bitcast.5, s32[1,24576]{1,0:T(1,128)} %bitcast.11, bf16[64,24576]{1,0:T(8,128)(2,1)} %bitcast.8), custom_call_target="tpu_custom_call" | custom-call | tf_op jit(solution)/shard_map/interior/pallas_call | solution.py:170
  41.3 0.0 collective-permute-done.low_ref
  41.3 0.0 copy-start
  41.3 0.0 collective-permute-done.1.high_ref
  41.3 0.0 copy-start.1
  41.4 0.7 copy-done
  42.1 0.1 copy-done.1
  42.2 6.9 %ends.1 = (f32[64,24576]{1,0:T(8,128)}, f32[64,128]{1,0:T(8,128)}) custom-call(bf16[272,640]{1,0:T(8,128)(2,1)} %copy-done, bf16[272,640]{1,0:T(8,128)(2,1)} %copy-done.1, f32[64,128]{1,0:T(8,128)} %get-tuple-element.12.sums_ref, s32[1,24576]{1,0:T(1,128)} %bitcast.12, bf16[192,24576]{1,0:T(8,128)(2,1)} %bitcast.6, ...), custom_call_target="tpu_custom_call", output_to_operand_aliasing={{0}: (6, {})} | custom-call | tf_op jit(solution)/shard_map/ends/pallas_call | solution.py:309
  49.0 3.8 %collective-permute-start.2 = (f32[64,128]{1,0:T(8,128)}, f32[64,128]{1,0:T(8,128)S(1)}, u32[]{:S(2)}, u32[]{:S(2)}) collective-permute-start(f32[64,128]{1,0:T(8,128)} %get-tuple-element.14), channel_id=1, source_target_pairs={{0,8},{8,0},{16,24},{24,16},{1,9},{9,1},{17,25},{25,17},{2,10},{10... | collective-permute-start | bytes 98312 | tf_op jit(solution)/shard_map/ppermute | solution.py:345
  52.9 1.1 %collective-permute-done.2 = f32[64,128]{1,0:T(8,128)S(1)} collective-permute-done((f32[64,128]{1,0:T(8,128)}, f32[64,128]{1,0:T(8,128)S(1)}, u32[]{:S(2)}, u32[]{:S(2)}) %collective-permute-start.2) | collective-permute-done | bytes 32800 | tf_op jit(solution)/shard_map/ppermute | solution.py:345
  53.9 0.8 add.15
  54.7 2.5 %collective-permute-start.3 = (f32[64,128]{1,0:T(8,128)S(1)}, f32[64,128]{1,0:T(8,128)S(1)}, u32[]{:S(2)}, u32[]{:S(2)}) collective-permute-start(f32[64,128]{1,0:T(8,128)S(1)} %add.15), channel_id=1, source_target_pairs={{0,16},{8,24},{16,0},{24,8},{1,17},{9,25},{17,1},{25,9},{2,18},{10... | collective-permute-start | bytes 98312 | tf_op jit(solution)/shard_map/ppermute | solution.py:345
  57.2 1.9 %collective-permute-done.3 = f32[64,128]{1,0:T(8,128)S(1)} collective-permute-done((f32[64,128]{1,0:T(8,128)S(1)}, f32[64,128]{1,0:T(8,128)S(1)}, u32[]{:S(2)}, u32[]{:S(2)}) %collective-permute-start.3) | collective-permute-done | bytes 32800 | tf_op jit(solution)/shard_map/ppermute | solution.py:345
  59.1 0.0 collective-permute-start.4
  59.1 3.9 %collective-permute-done.4 = f32[64,128]{1,0:T(8,128)S(1)} collective-permute-done((f32[64,128]{1,0:T(8,128)S(1)}, f32[64,128]{1,0:T(8,128)S(1)}, u32[]{:S(2)}, u32[]{:S(2)}) %collective-permute-start.4) | collective-permute-done | bytes 32800 | tf_op jit(solution)/shard_map/ppermute | solution.py:345
  63.0 0.0 collective-permute-start.5
  63.0 3.9 %collective-permute-done.5 = f32[64,128]{1,0:T(8,128)S(1)} collective-permute-done((f32[64,128]{1,0:T(8,128)S(1)}, f32[64,128]{1,0:T(8,128)S(1)}, u32[]{:S(2)}, u32[]{:S(2)}) %collective-permute-start.5) | collective-permute-done | bytes 32800 | tf_op jit(solution)/shard_map/ppermute | solution.py:345
  66.9 0.7 collective-permute-start.6
  67.6 4.1 %collective-permute-done.6 = f32[64,128]{1,0:T(8,128)S(1)} collective-permute-done((f32[64,128]{1,0:T(8,128)S(1)}, f32[64,128]{1,0:T(8,128)S(1)}, u32[]{:S(2)}, u32[]{:S(2)}) %collective-permute-start.6) | collective-permute-done | bytes 32800 | tf_op jit(solution)/shard_map/ppermute | solution.py:345
  71.7 0.6 add.19.gram_ref
  72.4 7.9 %basis.1 = (f32[64,24576]{1,0:T(8,128)}, f32[64,64]{1,0:T(8,128)}) custom-call(f32[64,128]{1,0:T(8,128)} %add.19.gram_ref, f32[64,24576]{1,0:T(8,128)} %get-tuple-element.15.level_hbm), custom_call_target="tpu_custom_call" | custom-call | tf_op jit(solution)/shard_map/basis/pallas_call | solution.py:396
  (3 shorter events, 0.0 us)
Async XLA Ops:
  2.7 38.6 %collective-permute-start = (bf16[272,640]{1,0:T(8,128)(2,1)}, bf16[272,640]{1,0:T(8,128)(2,1)S(1)}, u32[]{:S(2)}, u32[]{:S(2)}) collective-permute-start(bf16[272,640]{1,0:T(8,128)(2,1)} %get-tuple-element.10), channel_id=1, source_target_pairs={{0,1},{1,2},{2,3},{3,4},{4,5},{5,6},{6,7},{7,8},{8,9},{9,10},{10,1... | collective-permute-start | bytes 1044488 | tf_op jit(solution)/shard_map/ppermute | solution.py:423
  7.6 33.7 %collective-permute-start.1 = (bf16[272,640]{1,0:T(8,128)(2,1)}, bf16[272,640]{1,0:T(8,128)(2,1)S(1)}, u32[]{:S(2)}, u32[]{:S(2)}) collective-permute-start(bf16[272,640]{1,0:T(8,128)(2,1)} %get-tuple-element.11), channel_id=1, source_target_pairs={{1,0},{2,1},{3,2},{4,3},{5,4},{6,5},{7,6},{8,7},{9,8},{10,9},{11,1... | collective-permute-start | bytes 1044488 | tf_op jit(solution)/shard_map/ppermute | solution.py:424
  41.3 0.7 copy-start
  41.3 0.8 %copy-start.1 = (bf16[272,640]{1,0:T(8,128)(2,1)}, bf16[272,640]{1,0:T(8,128)(2,1)S(1)}, u32[]{:S(2)}) copy-start(bf16[272,640]{1,0:T(8,128)(2,1)S(1)} %collective-permute-done.1.high_ref) | copy-start | bytes 1044484
  49.0 4.9 %collective-permute-start.2 = (f32[64,128]{1,0:T(8,128)}, f32[64,128]{1,0:T(8,128)S(1)}, u32[]{:S(2)}, u32[]{:S(2)}) collective-permute-start(f32[64,128]{1,0:T(8,128)} %get-tuple-element.14), channel_id=1, source_target_pairs={{0,8},{8,0},{16,24},{24,16},{1,9},{9,1},{17,25},{25,17},{2,10},{10... | collective-permute-start | bytes 98312 | tf_op jit(solution)/shard_map/ppermute | solution.py:345
  54.7 4.4 %collective-permute-start.3 = (f32[64,128]{1,0:T(8,128)S(1)}, f32[64,128]{1,0:T(8,128)S(1)}, u32[]{:S(2)}, u32[]{:S(2)}) collective-permute-start(f32[64,128]{1,0:T(8,128)S(1)} %add.15), channel_id=1, source_target_pairs={{0,16},{8,24},{16,0},{24,8},{1,17},{9,25},{17,1},{25,9},{2,18},{10... | collective-permute-start | bytes 98312 | tf_op jit(solution)/shard_map/ppermute | solution.py:345
  59.1 3.9 %collective-permute-start.4 = (f32[64,128]{1,0:T(8,128)S(1)}, f32[64,128]{1,0:T(8,128)S(1)}, u32[]{:S(2)}, u32[]{:S(2)}) collective-permute-start(f32[64,128]{1,0:T(8,128)S(1)} %add.16), channel_id=1, source_target_pairs={{0,1},{1,0},{2,3},{3,2},{4,5},{5,4},{6,7},{7,6},{8,9},{9,8},{10,11... | collective-permute-start | bytes 98312 | tf_op jit(solution)/shard_map/ppermute | solution.py:345
  63.0 3.9 %collective-permute-start.5 = (f32[64,128]{1,0:T(8,128)S(1)}, f32[64,128]{1,0:T(8,128)S(1)}, u32[]{:S(2)}, u32[]{:S(2)}) collective-permute-start(f32[64,128]{1,0:T(8,128)S(1)} %add.17), channel_id=1, source_target_pairs={{0,2},{1,3},{2,0},{3,1},{4,6},{5,7},{6,4},{7,5},{8,10},{9,11},{10,... | collective-permute-start | bytes 98312 | tf_op jit(solution)/shard_map/ppermute | solution.py:345
  66.9 4.8 %collective-permute-start.6 = (f32[64,128]{1,0:T(8,128)S(1)}, f32[64,128]{1,0:T(8,128)S(1)}, u32[]{:S(2)}, u32[]{:S(2)}) collective-permute-start(f32[64,128]{1,0:T(8,128)S(1)} %add.18), channel_id=1, source_target_pairs={{0,4},{1,5},{2,6},{3,7},{4,0},{5,1},{6,2},{7,3},{8,12},{9,13},{10,... | collective-permute-start | bytes 98312 | tf_op jit(solution)/shard_map/ppermute | solution.py:345

commit v7 on v6

--- a/solution.py
+++ b/solution.py
@@ -335,15 +335,20 @@
 
 
 def total(x, axes):
-    for axis in axes:
-        size = lax.axis_size(axis)
-        if size & (size - 1):
-            x = lax.psum(x, axis)
-            continue
-        stride = 1
-        while stride < size:
-            x = x + lax.ppermute(x, axis, [(i, i ^ stride) for i in range(size)])
-            stride *= 2
+    size = lax.axis_size(axes)
+    minor = lax.axis_size(axes[-1])
+    if size & (size - 1):
+        return lax.psum(x, axes)
+
+    def partner(bits):
+        return lax.ppermute(x, axes, [(i, i ^ bits) for i in range(size)])
+
+    strides = [1 << k for k in range(size.bit_length() - 1)]
+    strides = [s for s in strides if s >= minor] + [s for s in strides if s < minor]
+    if len(strides) % 2:
+        x = x + partner(strides.pop(0))
+    for one, two in zip(strides[::2], strides[1::2]):
+        x = (x + partner(one)) + (partner(two) + partner(one ^ two))
     return x
 
 

time: 80.8 us -> 78.4 us (0.970)
  waiting for transfers between devices: 14.9 us -> 7.2 us
  starting transfers between devices: 13.2 us -> 18.4 us
    ppermute x5 -> x7, waiting for transfers between devices: 14.9 us -> 7.2 us  [partner(): return lax.ppermute(x, axes, [(i, i ^ bits) for i in range(size)])]
    ppermute x5 -> x7, starting transfers between devices: 7.03 us -> 12.2 us  [partner(): return lax.ppermute(x, axes, [(i, i ^ bits) for i in range(size)])]
  transfers between devices with their start and end apart: 7 -> 9, of which waited for: 5 -> 7; matrix products, arithmetic and copies ran while one was open for 0% -> 0% of each run, Pallas kernels for 40% -> 41%
where the time goes in v7:
time: 78.4 us; the launch traced here: 78 us
  Pallas kernels  49.3 us (63%)
  starting transfers between devices  18.4 us (23%)
  waiting for transfers between devices  7.2 us (9%)
  other arithmetic  1.39 us (2%)
  between operations  0.87 us (1%)
  local copies, waits for them, and re-layouts  0.82 us (1%)
    pallas_call x1, Pallas kernels, interior(): pl.pallas_call(interior_kernel, grid=(rows // CHUNK,), in_specs=[pl.Block...  32.4 us
    ppermute x7, starting transfers between devices, partner(): return lax.ppermute(x, axes, [(i, i ^ bits) for i in range(size)])  12.2 us
    pallas_call x1, Pallas kernels, orthonormal(): pl.pallas_call(basis_kernel, grid=(rows // width,), in_specs=[whole, pl.B...  7.94 us
    ppermute x7, waiting for transfers between devices, partner(): return lax.ppermute(x, axes, [(i, i ^ bits) for i in range(size)])  7.2 us
    pallas_call x1, Pallas kernels, ends(): pl.pallas_call(ends_kernel, in_specs=[whole, whole, whole, away, away, aw...  6.85 us
    ppermute x1, starting transfers between devices, per_device(): low = lax.ppermute(last, axes, [(i, i + 1) for i in steps])  4.89 us
    pallas_call x1, Pallas kernels, edges(): pl.pallas_call(edges_kernel, in_specs=[away, away, away], out_specs=[whol...  2.12 us
  transfers between devices with their start and end apart: 9, of which 7 were waited for; matrix products, arithmetic and copies ran while one was open for 0% of the time, Pallas kernels for 41%

profile of v7, /device:TPU:0, one launch (start us, length us, event | category | flops | bytes accessed | tf_op | source)
XLA Modules:
  0.0 78.0 jit_solution(3413766520109272500)
XLA Ops:
  0.6 2.1 %edges.1 = (bf16[272,640]{1,0:T(8,128)(2,1)}, bf16[272,640]{1,0:T(8,128)(2,1)}) custom-call(bf16[192,24576]{1,0:T(8,128)(2,1)} %bitcast.4, s32[1,24576]{1,0:T(1,128)} %bitcast.10, bf16[64,24576]{1,0:T(8,128)(2,1)} %bitcast.7), custom_call_target="tpu_custom_call" | custom-call | tf_op jit(solution)/shard_map/edges/pallas_call | solution.py:224
  2.8 4.9 %collective-permute-start = (bf16[272,640]{1,0:T(8,128)(2,1)}, bf16[272,640]{1,0:T(8,128)(2,1)S(1)}, u32[]{:S(2)}, u32[]{:S(2)}) collective-permute-start(bf16[272,640]{1,0:T(8,128)(2,1)} %get-tuple-element.10), channel_id=1, source_target_pairs={{0,1},{1,2},{2,3},{3,4},{4,5},{5,6},{6,7},{7,8},{8,9},{9,10},{10,1... | collective-permute-start | bytes 1044488 | tf_op jit(solution)/shard_map/ppermute | solution.py:428
  7.7 1.3 %collective-permute-start.1 = (bf16[272,640]{1,0:T(8,128)(2,1)}, bf16[272,640]{1,0:T(8,128)(2,1)S(1)}, u32[]{:S(2)}, u32[]{:S(2)}) collective-permute-start(bf16[272,640]{1,0:T(8,128)(2,1)} %get-tuple-element.11), channel_id=1, source_target_pairs={{1,0},{2,1},{3,2},{4,3},{5,4},{6,5},{7,6},{8,7},{9,8},{10,9},{11,1... | collective-permute-start | bytes 1044488 | tf_op jit(solution)/shard_map/ppermute | solution.py:429
  9.0 32.4 %interior.1 = (f32[64,24576]{1,0:T(8,128)}, f32[64,128]{1,0:T(8,128)}) custom-call(bf16[192,24576]{1,0:T(8,128)(2,1)} %bitcast.5, s32[1,24576]{1,0:T(1,128)} %bitcast.11, bf16[64,24576]{1,0:T(8,128)(2,1)} %bitcast.8), custom_call_target="tpu_custom_call" | custom-call | tf_op jit(solution)/shard_map/interior/pallas_call | solution.py:170
  41.3 0.0 collective-permute-done.low_ref
  41.4 0.0 copy-start.1
  41.4 0.7 copy-done
  42.1 0.1 copy-done.1
  42.2 6.8 %ends.1 = (f32[64,24576]{1,0:T(8,128)}, f32[64,128]{1,0:T(8,128)}) custom-call(bf16[272,640]{1,0:T(8,128)(2,1)} %copy-done, bf16[272,640]{1,0:T(8,128)(2,1)} %copy-done.1, f32[64,128]{1,0:T(8,128)} %get-tuple-element.12.sums_ref, s32[1,24576]{1,0:T(1,128)} %bitcast.12, bf16[192,24576]{1,0:T(8,128)(2,1)} %bitcast.6, ...), custom_call_target="tpu_custom_call", output_to_operand_aliasing={{0}: (6, {})} | custom-call | tf_op jit(solution)/shard_map/ends/pallas_call | solution.py:309
  49.0 3.8 %collective-permute-start.2 = (f32[64,128]{1,0:T(8,128)}, f32[64,128]{1,0:T(8,128)S(1)}, u32[]{:S(2)}, u32[]{:S(2)}) collective-permute-start(f32[64,128]{1,0:T(8,128)} %get-tuple-element.14), channel_id=1, source_target_pairs={{0,8},{1,9},{2,10},{3,11},{4,12},{5,13},{6,14},{7,15},{8,0},{9,1},... | collective-permute-start | bytes 98312 | tf_op jit(solution)/shard_map/ppermute | solution.py:344
  52.9 1.1 %collective-permute-done.2 = f32[64,128]{1,0:T(8,128)S(1)} collective-permute-done((f32[64,128]{1,0:T(8,128)}, f32[64,128]{1,0:T(8,128)S(1)}, u32[]{:S(2)}, u32[]{:S(2)}) %collective-permute-start.2) | collective-permute-done | bytes 32800 | tf_op jit(solution)/shard_map/ppermute | solution.py:344
  53.9 0.8 add.21
  54.7 0.1 collective-permute-start.5
  54.8 3.8 %collective-permute-start.4 = (f32[64,128]{1,0:T(8,128)S(1)}, f32[64,128]{1,0:T(8,128)S(1)}, u32[]{:S(2)}, u32[]{:S(2)}) collective-permute-start(f32[64,128]{1,0:T(8,128)S(1)} %add.21), channel_id=1, source_target_pairs={{0,1},{1,0},{2,3},{3,2},{4,5},{5,4},{6,7},{7,6},{8,9},{9,8},{10,11... | collective-permute-start | bytes 98312 | tf_op jit(solution)/shard_map/ppermute | solution.py:344
  58.7 0.9 %collective-permute-done.5 = f32[64,128]{1,0:T(8,128)S(1)} collective-permute-done((f32[64,128]{1,0:T(8,128)S(1)}, f32[64,128]{1,0:T(8,128)S(1)}, u32[]{:S(2)}, u32[]{:S(2)}) %collective-permute-start.5) | collective-permute-done | bytes 32800 | tf_op jit(solution)/shard_map/ppermute | solution.py:344
  59.5 1.0 %collective-permute-done.4 = f32[64,128]{1,0:T(8,128)S(1)} collective-permute-done((f32[64,128]{1,0:T(8,128)S(1)}, f32[64,128]{1,0:T(8,128)S(1)}, u32[]{:S(2)}, u32[]{:S(2)}) %collective-permute-start.4) | collective-permute-done | bytes 32800 | tf_op jit(solution)/shard_map/ppermute | solution.py:344
  60.6 2.0 %collective-permute-done.3 = f32[64,128]{1,0:T(8,128)S(1)} collective-permute-done((f32[64,128]{1,0:T(8,128)S(1)}, f32[64,128]{1,0:T(8,128)S(1)}, u32[]{:S(2)}, u32[]{:S(2)}) %collective-permute-start.3) | collective-permute-done | bytes 32800 | tf_op jit(solution)/shard_map/ppermute | solution.py:344
  62.6 1.3 %collective-permute-start.8 = (f32[64,128]{1,0:T(8,128)S(1)}, f32[64,128]{1,0:T(8,128)S(1)}, u32[]{:S(2)}, u32[]{:S(2)}) collective-permute-start(f32[64,128]{1,0:T(8,128)S(1)} %add_add_fusion.1), channel_id=1, source_target_pairs={{0,6},{1,7},{2,4},{3,5},{4,2},{5,3},{6,0},{7,1},{8,14},{9,15},{10,... | collective-permute-start | bytes 98312 | tf_op jit(solution)/shard_map/ppermute | solution.py:344
  63.9 3.2 %collective-permute-start.6 = (f32[64,128]{1,0:T(8,128)S(1)}, f32[64,128]{1,0:T(8,128)S(1)}, u32[]{:S(2)}, u32[]{:S(2)}) collective-permute-start(f32[64,128]{1,0:T(8,128)S(1)} %add_add_fusion.1), channel_id=1, source_target_pairs={{0,2},{1,3},{2,0},{3,1},{4,6},{5,7},{6,4},{7,5},{8,10},{9,11},{10,... | collective-permute-start | bytes 98312 | tf_op jit(solution)/shard_map/ppermute | solution.py:344
  67.0 1.3 %collective-permute-done.8 = f32[64,128]{1,0:T(8,128)S(1)} collective-permute-done((f32[64,128]{1,0:T(8,128)S(1)}, f32[64,128]{1,0:T(8,128)S(1)}, u32[]{:S(2)}, u32[]{:S(2)}) %collective-permute-start.8) | collective-permute-done | bytes 32800 | tf_op jit(solution)/shard_map/ppermute | solution.py:344
  68.4 0.8 %collective-permute-done.7 = f32[64,128]{1,0:T(8,128)S(1)} collective-permute-done((f32[64,128]{1,0:T(8,128)S(1)}, f32[64,128]{1,0:T(8,128)S(1)}, u32[]{:S(2)}, u32[]{:S(2)}) %collective-permute-start.7) | collective-permute-done | bytes 32800 | tf_op jit(solution)/shard_map/ppermute | solution.py:344
  69.2 0.1 collective-permute-done.6
  69.3 0.6 add_add_fusion.gram_ref
  69.9 7.9 %basis.1 = (f32[64,24576]{1,0:T(8,128)}, f32[64,64]{1,0:T(8,128)}) custom-call(f32[64,128]{1,0:T(8,128)} %add_add_fusion.gram_ref, f32[64,24576]{1,0:T(8,128)} %get-tuple-element.15.level_hbm), custom_call_target="tpu_custom_call" | custom-call | tf_op jit(solution)/shard_map/basis/pallas_call | solution.py:401
  (5 shorter events, 0.0 us)
Async XLA Ops:
  2.8 38.6 %collective-permute-start = (bf16[272,640]{1,0:T(8,128)(2,1)}, bf16[272,640]{1,0:T(8,128)(2,1)S(1)}, u32[]{:S(2)}, u32[]{:S(2)}) collective-permute-start(bf16[272,640]{1,0:T(8,128)(2,1)} %get-tuple-element.10), channel_id=1, source_target_pairs={{0,1},{1,2},{2,3},{3,4},{4,5},{5,6},{6,7},{7,8},{8,9},{9,10},{10,1... | collective-permute-start | bytes 1044488 | tf_op jit(solution)/shard_map/ppermute | solution.py:428
  7.7 33.7 %collective-permute-start.1 = (bf16[272,640]{1,0:T(8,128)(2,1)}, bf16[272,640]{1,0:T(8,128)(2,1)S(1)}, u32[]{:S(2)}, u32[]{:S(2)}) collective-permute-start(bf16[272,640]{1,0:T(8,128)(2,1)} %get-tuple-element.11), channel_id=1, source_target_pairs={{1,0},{2,1},{3,2},{4,3},{5,4},{6,5},{7,6},{8,7},{9,8},{10,9},{11,1... | collective-permute-start | bytes 1044488 | tf_op jit(solution)/shard_map/ppermute | solution.py:429
  41.3 0.8 copy-start
  41.4 0.8 %copy-start.1 = (bf16[272,640]{1,0:T(8,128)(2,1)}, bf16[272,640]{1,0:T(8,128)(2,1)S(1)}, u32[]{:S(2)}) copy-start(bf16[272,640]{1,0:T(8,128)(2,1)S(1)} %collective-permute-done.1.high_ref) | copy-start | bytes 1044484
  49.0 4.9 %collective-permute-start.2 = (f32[64,128]{1,0:T(8,128)}, f32[64,128]{1,0:T(8,128)S(1)}, u32[]{:S(2)}, u32[]{:S(2)}) collective-permute-start(f32[64,128]{1,0:T(8,128)} %get-tuple-element.14), channel_id=1, source_target_pairs={{0,8},{1,9},{2,10},{3,11},{4,12},{5,13},{6,14},{7,15},{8,0},{9,1},... | collective-permute-start | bytes 98312 | tf_op jit(solution)/shard_map/ppermute | solution.py:344
  54.7 4.8 %collective-permute-start.5 = (f32[64,128]{1,0:T(8,128)S(1)}, f32[64,128]{1,0:T(8,128)S(1)}, u32[]{:S(2)}, u32[]{:S(2)}) collective-permute-start(f32[64,128]{1,0:T(8,128)S(1)} %add.21), channel_id=1, source_target_pairs={{0,17},{1,16},{2,19},{3,18},{4,21},{5,20},{6,23},{7,22},{8,25},{9,... | collective-permute-start | bytes 98312 | tf_op jit(solution)/shard_map/ppermute | solution.py:344
  54.8 5.7 %collective-permute-start.4 = (f32[64,128]{1,0:T(8,128)S(1)}, f32[64,128]{1,0:T(8,128)S(1)}, u32[]{:S(2)}, u32[]{:S(2)}) collective-permute-start(f32[64,128]{1,0:T(8,128)S(1)} %add.21), channel_id=1, source_target_pairs={{0,1},{1,0},{2,3},{3,2},{4,5},{5,4},{6,7},{7,6},{8,9},{9,8},{10,11... | collective-permute-start | bytes 98312 | tf_op jit(solution)/shard_map/ppermute | solution.py:344
  58.7 3.9 %collective-permute-start.3 = (f32[64,128]{1,0:T(8,128)S(1)}, f32[64,128]{1,0:T(8,128)S(1)}, u32[]{:S(2)}, u32[]{:S(2)}) collective-permute-start(f32[64,128]{1,0:T(8,128)S(1)} %add.21), channel_id=1, source_target_pairs={{0,16},{1,17},{2,18},{3,19},{4,20},{5,21},{6,22},{7,23},{8,24},{9,... | collective-permute-start | bytes 98312 | tf_op jit(solution)/shard_map/ppermute | solution.py:344
  62.6 5.8 %collective-permute-start.8 = (f32[64,128]{1,0:T(8,128)S(1)}, f32[64,128]{1,0:T(8,128)S(1)}, u32[]{:S(2)}, u32[]{:S(2)}) collective-permute-start(f32[64,128]{1,0:T(8,128)S(1)} %add_add_fusion.1), channel_id=1, source_target_pairs={{0,6},{1,7},{2,4},{3,5},{4,2},{5,3},{6,0},{7,1},{8,14},{9,15},{10,... | collective-permute-start | bytes 98312 | tf_op jit(solution)/shard_map/ppermute | solution.py:344
  63.8 5.3 %collective-permute-start.7 = (f32[64,128]{1,0:T(8,128)S(1)}, f32[64,128]{1,0:T(8,128)S(1)}, u32[]{:S(2)}, u32[]{:S(2)}) collective-permute-start(f32[64,128]{1,0:T(8,128)S(1)} %add_add_fusion.1), channel_id=1, source_target_pairs={{0,4},{1,5},{2,6},{3,7},{4,0},{5,1},{6,2},{7,3},{8,12},{9,13},{10,... | collective-permute-start | bytes 98312 | tf_op jit(solution)/shard_map/ppermute | solution.py:344
  63.9 5.4 %collective-permute-start.6 = (f32[64,128]{1,0:T(8,128)S(1)}, f32[64,128]{1,0:T(8,128)S(1)}, u32[]{:S(2)}, u32[]{:S(2)}) collective-permute-start(f32[64,128]{1,0:T(8,128)S(1)} %add_add_fusion.1), channel_id=1, source_target_pairs={{0,2},{1,3},{2,0},{3,1},{4,6},{5,7},{6,4},{7,5},{8,10},{9,11},{10,... | collective-permute-start | bytes 98312 | tf_op jit(solution)/shard_map/ppermute | solution.py:344
